TPU v7x, 32 devices: a whole 2x2x4 slice. The times are simulated.
32 devices in a mesh: dp: 16 (over z, x, core), section: 2 (over y).
Axes of the slice: x: 2, y: 2, z: 4, core: 2. Of those that a mesh axis runs over, the one named last changes fastest.
Arguments:
- section_inputs: bfloat16 [2, 128, 8, 4, 4, 768], P('section', 'dp'), may hold values from -6 to 6
- cotangent: bfloat16 [128, 8, 4, 4, 128], P('dp'), may hold values from -6 to 6
- sessions: int32 [128], P('dp'), may hold values from 0 to 3
- point_weight: bfloat16 [2, 768, 768], P('section', 'dp'), may hold values from -0.21875 to 0.21875
- spatial_kernel: float32 [2, 9, 768], P('section'), may hold values from -1.5 to 1.5
- temporal_kernel: float32 [2, 5, 768], P('section'), may hold values from -2 to 2
- readout: bfloat16 [4, 128, 768], replicated, may hold values from -0.5 to 0.5
Outputs:
- point_grads: float32 [2, 768, 768], P('section', 'dp')
- spatial_grads: float32 [2, 9, 768], P('section')
- temporal_grads: float32 [2, 5, 768], P('section')
All inputs are finite; a program needn't handle non-finite values.
Results may differ from a plain program's by a relative error of at most 0.0071.
Values may be sent and summed in bfloat16 or wider, within the bound.
A program may use at most 64 MiB of HBM per device.

v0:
```python
import math

import jax
import jax.numpy as jnp
from jax import lax
from jax.sharding import PartitionSpec as P

INV_ROOT_TWO = 0.7071067811865476
INV_ROOT_TAU = 0.3989422804014327


def from_behind(block, axis, distance):
    devices = range(lax.axis_size(axis))
    route = [(i - distance, i) for i in devices if i - distance in devices]
    return lax.ppermute(block, axis, route)


def gelu_value(pre_act):
    return 0.5 * pre_act * (1.0 + jax.scipy.special.erf(pre_act * INV_ROOT_TWO))


def gelu_slope(pre_act):
    return (
        0.5 * (1.0 + jax.scipy.special.erf(pre_act * INV_ROOT_TWO))
        + pre_act * jnp.exp(-0.5 * pre_act * pre_act) * INV_ROOT_TAU
    )


def spatial_pad(field_in):
    pad_spec = [(0, 0)] * (field_in.ndim - 3) + [(1, 1), (1, 1), (0, 0)]
    return jnp.pad(field_in, pad_spec)


def spatial(field_in, kernel):
    height, width = (field_in.shape[-3], field_in.shape[-2])
    padded = spatial_pad(field_in)
    summed = jnp.zeros_like(field_in)
    for row_off in range(3):
        for col_off in range(3):
            summed = (
                summed
                + kernel[3 * row_off + col_off]
                * padded[..., row_off : row_off + height, col_off : col_off + width, :]
            )
    return summed


def spatial_back(grad_in, kernel):
    height, width = (grad_in.shape[-3], grad_in.shape[-2])
    padded = spatial_pad(grad_in)
    summed = jnp.zeros_like(grad_in)
    for row_off in range(3):
        for col_off in range(3):
            summed = (
                summed
                + kernel[3 * row_off + col_off]
                * padded[
                    ..., 2 - row_off : 2 - row_off + height, 2 - col_off : 2 - col_off + width, :
                ]
            )
    return summed


def spatial_kernel_grad(field_in, grad_in):
    height, width = (field_in.shape[-3], field_in.shape[-2])
    padded = spatial_pad(field_in)
    axes_all = tuple(range(field_in.ndim - 1))
    parts = []
    for row_off in range(3):
        for col_off in range(3):
            parts.append(
                jnp.sum(
                    padded[..., row_off : row_off + height, col_off : col_off + width, :] * grad_in,
                    axis=axes_all,
                )
            )
    return jnp.stack(parts)


def front_pad(field_in, tap_count):
    pad_spec = [(0, 0)] * (field_in.ndim - 4) + [(tap_count - 1, 0), (0, 0), (0, 0), (0, 0)]
    return jnp.pad(field_in, pad_spec)


def temporal(field_in, kernel):
    tap_count = kernel.shape[0]
    frames = field_in.shape[-4]
    padded = front_pad(field_in, tap_count)
    summed = jnp.zeros_like(field_in)
    for delay in range(tap_count):
        first = tap_count - 1 - delay
        summed = summed + kernel[delay] * padded[..., first : first + frames, :, :, :]
    return summed


def temporal_back(grad_in, kernel):
    tap_count = kernel.shape[0]
    frames = grad_in.shape[-4]
    pad_spec = [(0, 0)] * (grad_in.ndim - 4) + [(0, tap_count - 1), (0, 0), (0, 0), (0, 0)]
    padded = jnp.pad(grad_in, pad_spec)
    summed = jnp.zeros_like(grad_in)
    for delay in range(tap_count):
        summed = summed + kernel[delay] * padded[..., delay : delay + frames, :, :, :]
    return summed


def temporal_kernel_grad(field_in, grad_in, tap_count):
    frames = field_in.shape[-4]
    padded = front_pad(field_in, tap_count)
    axes_all = tuple(range(field_in.ndim - 1))
    parts = []
    for delay in range(tap_count):
        first = tap_count - 1 - delay
        parts.append(jnp.sum(padded[..., first : first + frames, :, :, :] * grad_in, axis=axes_all))
    return jnp.stack(parts)


def section_back(inputs, grad_out, s_kernel, t_kernel, hidden_of):
    field_in = inputs.astype(jnp.float32)
    spread = spatial(field_in, s_kernel)
    pre_act = temporal(spread, t_kernel)
    hidden = gelu_value(pre_act).astype(jnp.bfloat16)
    channels = inputs.shape[-1]
    flat_grad = grad_out.reshape(-1, channels)
    flat_hidden = hidden.reshape(-1, channels)
    hidden_grad = hidden_of(flat_grad).reshape(pre_act.shape)
    pre_grad = hidden_grad * gelu_slope(pre_act)
    spread_grad = temporal_back(pre_grad, t_kernel)
    in_grad = (grad_out.astype(jnp.float32) + spatial_back(spread_grad, s_kernel)).astype(
        jnp.bfloat16
    )
    weight_grad = jnp.dot(flat_hidden.T, flat_grad, preferred_element_type=jnp.float32)
    s_part = spatial_kernel_grad(field_in, spread_grad)
    t_part = temporal_kernel_grad(spread, pre_grad, t_kernel.shape[0])
    return (in_grad, weight_grad, s_part, t_part)


def local(
    section_inputs, cotangent, sessions, point_weight, spatial_kernel, temporal_kernel, readout
):
    section_count = lax.axis_size("section")
    my_section = lax.axis_index("section")
    inputs = section_inputs[0]
    s_kernel = spatial_kernel[0]
    t_kernel = temporal_kernel[0]
    weight_shard = point_weight[0]
    clip_count = inputs.shape[0]
    channels = inputs.shape[-1]
    chosen = jnp.take(readout, sessions, axis=0)
    top_grads = jnp.einsum(
        "cfhwr,crk->cfhwk", cotangent, chosen, preferred_element_type=jnp.float32
    ).astype(jnp.bfloat16)
    block_size = 2
    step_count = clip_count // block_size
    tick_count = step_count + section_count - 1
    full_weight = lax.all_gather(weight_shard, "dp", axis=0, tiled=True)

    def hidden_of(flat_grad):
        return jnp.dot(flat_grad, full_weight.T, preferred_element_type=jnp.float32)

    block_shape = (block_size,) + inputs.shape[1:]

    def tick(tick_index, state_now):
        incoming, w_sum, s_sum, t_sum = state_now
        clip_step = tick_index - (section_count - 1 - my_section)
        is_live = (clip_step >= 0) & (clip_step < step_count)
        first_clip = jnp.clip(clip_step, 0, step_count - 1) * block_size
        inputs_block = lax.dynamic_slice_in_dim(inputs, first_clip, block_size, 0)
        top_block = lax.dynamic_slice_in_dim(top_grads, first_clip, block_size, 0)
        grad_out = jnp.where(my_section == section_count - 1, top_block, incoming)

        def live_work(sums):
            in_grad, w_part, s_part, t_part = section_back(
                inputs_block, grad_out, s_kernel, t_kernel, hidden_of
            )
            return (in_grad, sums[0] + w_part, sums[1] + s_part, sums[2] + t_part)

        def dead_work(sums):
            return (jnp.zeros(block_shape, jnp.bfloat16), sums[0], sums[1], sums[2])

        in_grad, w_new, s_new, t_new = lax.cond(
            is_live, live_work, dead_work, (w_sum, s_sum, t_sum)
        )
        passed = from_behind(in_grad, "section", -1)
        return (passed, w_new, s_new, t_new)

    start_state = (
        jnp.zeros(block_shape, jnp.bfloat16),
        jnp.zeros((channels, channels), jnp.float32),
        jnp.zeros((9, channels), jnp.float32),
        jnp.zeros(t_kernel.shape, jnp.float32),
    )
    finals = lax.fori_loop(0, tick_count, tick, start_state)
    weight_grads = lax.psum_scatter(finals[1], "dp", scatter_dimension=0, tiled=True)
    s_total, t_total = lax.psum((finals[2], finals[3]), "dp")
    rows_all = (
        clip_count * lax.axis_size("dp") * inputs.shape[1] * inputs.shape[2] * inputs.shape[3]
    )
    factor = 1.0 / math.sqrt(rows_all)
    return ((weight_grads * factor)[None], (s_total * factor)[None], (t_total * factor)[None])


def solution(mesh):
    return jax.shard_map(
        local,
        mesh=mesh,
        in_specs=(
            P("section", "dp", None, None, None, None),
            P("dp", None, None, None, None),
            P("dp"),
            P("section", "dp", None),
            P("section", None, None),
            P("section", None, None),
            P(),
        ),
        out_specs=(P("section", "dp", None), P("section", None, None), P("section", None, None)),
        check_vma=False,
    )
```

profile of v0, /device:TPU:0, one launch (start us, length us, event | category | flops | bytes accessed | tf_op | source)
XLA Modules:
  0.0 254.5 jit_solution(1457571173146096510)
XLA Ops:
  10.7 3.1 %copy.22 = bf16[1,8,8,4,4,768]{5,2,4,3,1,0:T(8,128)(2,1)} copy(bf16[1,8,8,4,4,768]{5,4,3,2,1,0:T(4,128)(2,1)} %param.11) | data formatting | bytes 3145728 | tf_op args[0]
  16.5 34.8 %all-gather.3.cloned.1.call-done = bf16[1,768,768]{2,1,0:T(8,128)(2,1)} async-done(((bf16[1,48,768]{2,1,0:T(8,128)(2,1)}), bf16[1,768,768]{2,1,0:T(8,128)(2,1)}) %all-gather.3.cloned.1.call-update) | async-done | bytes 1179664 | tf_op jit(solution)/shard_map/all_gather | solution.py:156
  54.2 130.3 %while.21 = (s32[]{:T(128)}, bf16[2,8,4,4,768]{4,1,3,2,0:T(8,128)(2,1)S(1)}, f32[768,768]{1,0:T(8,128)}, f32[9,768]{1,0:T(8,128)}, f32[5,768]{1,0:T(8,128)}, /*i...) while((s32[]{:T(128)}, ...), condition=%wide.region_17.18_spmd, body=%wide.region_0.17_spmd.sunk | while | flops 625999872 | bytes 24124888 | solution.py:193
  55.5 25.5 %collective-permute-done = bf16[2,8,4,4,768]{4,1,3,2,0:T(8,128)(2,1)S(1)} collective-permute-done((bf16[2,8,4,4,768]{4,1,3,2,0:T(8,128)(2,1)S(1)}, bf16[2,8,4,4,768]{4,1,3,2,0:T(8,128)(2,1)S(1)}, u32[]{:S(2)}, u32[]{:S(2)}) %collective-permute-start) | collective-permute-done | bytes 393248 | tf_op jit(solution)/shard_map/while/body/eval_jaxpr/ppermute | solution.py:15
  81.0 14.6 %conditional.2 = (bf16[2,8,4,4,768]{4,1,3,2,0:T(8,128)(2,1)S(1)}, f32[768,768]{1,0:T(8,128)}, f32[9,768]{1,0:T(8,128)}, f32[5,768]{1,0:T(8,128)}) conditional(s32[]{:T(128)} %convert_element_type.67, (f32[768,768]{1,0:T(8,128)}, f32[9,768]{1,0:T(8,128)}, f32[5,768]{1,0:T(8,128)}) %tuple.101, (pred[]{:T(512)}, s32[]{:T(128)}, ...), branch_computations={%region_1.1_spmd, %region_2.16_spmd} | conditional | flops 625999872 | bytes 22551692 | solution.py:181
  83.9 2.1 multiply_reduce_fusion
  86.0 1.9 multiply_reduce_fusion.5
  91.5 4.1 %bitcast_add_fusion = f32[768,768]{1,0:T(8,128)} fusion(f32[768,768]{1,0:T(8,128)} %get-tuple-element.418, bf16[2,8,4,4,768]{4,1,3,2,0:T(8,128)(2,1)S(1)} %get-tuple-element.504, f32[2,8,4,4,768]{4,1,3,2,0:T(8,128)S(1)} %multiply_add_fusion.1, f32[768]{0:T(1024)S(1)} %get-tuple-element.471, f32[768]{0:T(1024)S(1)} %get-tuple-element.472, ...), kind=kOutput, calls=%fused_computation.25 | convolution fusion | flops 305332224 | bytes 5913600 | tf_op jit(solution)/shard_map/while/body/eval_jaxpr/cond/branch_1_fun/dot_general | solution.py:132
  96.9 11.4 %collective-permute-done = bf16[2,8,4,4,768]{4,1,3,2,0:T(8,128)(2,1)S(1)} collective-permute-done((bf16[2,8,4,4,768]{4,1,3,2,0:T(8,128)(2,1)S(1)}, bf16[2,8,4,4,768]{4,1,3,2,0:T(8,128)(2,1)S(1)}, u32[]{:S(2)}, u32[]{:S(2)}) %collective-permute-start) | collective-permute-done | bytes 393248 | tf_op jit(solution)/shard_map/while/body/eval_jaxpr/ppermute | solution.py:15
  108.2 14.6 %conditional.2 = (bf16[2,8,4,4,768]{4,1,3,2,0:T(8,128)(2,1)S(1)}, f32[768,768]{1,0:T(8,128)}, f32[9,768]{1,0:T(8,128)}, f32[5,768]{1,0:T(8,128)}) conditional(s32[]{:T(128)} %convert_element_type.67, (f32[768,768]{1,0:T(8,128)}, f32[9,768]{1,0:T(8,128)}, f32[5,768]{1,0:T(8,128)}) %tuple.101, (pred[]{:T(512)}, s32[]{:T(128)}, ...), branch_computations={%region_1.1_spmd, %region_2.16_spmd} | conditional | flops 625999872 | bytes 22551692 | solution.py:181
  111.2 2.1 multiply_reduce_fusion
  113.2 1.9 multiply_reduce_fusion.5
  118.7 4.1 %bitcast_add_fusion = f32[768,768]{1,0:T(8,128)} fusion(f32[768,768]{1,0:T(8,128)} %get-tuple-element.418, bf16[2,8,4,4,768]{4,1,3,2,0:T(8,128)(2,1)S(1)} %get-tuple-element.504, f32[2,8,4,4,768]{4,1,3,2,0:T(8,128)S(1)} %multiply_add_fusion.1, f32[768]{0:T(1024)S(1)} %get-tuple-element.471, f32[768]{0:T(1024)S(1)} %get-tuple-element.472, ...), kind=kOutput, calls=%fused_computation.25 | convolution fusion | flops 305332224 | bytes 5913600 | tf_op jit(solution)/shard_map/while/body/eval_jaxpr/cond/branch_1_fun/dot_general | solution.py:132
  124.1 10.5 %collective-permute-done = bf16[2,8,4,4,768]{4,1,3,2,0:T(8,128)(2,1)S(1)} collective-permute-done((bf16[2,8,4,4,768]{4,1,3,2,0:T(8,128)(2,1)S(1)}, bf16[2,8,4,4,768]{4,1,3,2,0:T(8,128)(2,1)S(1)}, u32[]{:S(2)}, u32[]{:S(2)}) %collective-permute-start) | collective-permute-done | bytes 393248 | tf_op jit(solution)/shard_map/while/body/eval_jaxpr/ppermute | solution.py:15
  134.6 14.6 %conditional.2 = (bf16[2,8,4,4,768]{4,1,3,2,0:T(8,128)(2,1)S(1)}, f32[768,768]{1,0:T(8,128)}, f32[9,768]{1,0:T(8,128)}, f32[5,768]{1,0:T(8,128)}) conditional(s32[]{:T(128)} %convert_element_type.67, (f32[768,768]{1,0:T(8,128)}, f32[9,768]{1,0:T(8,128)}, f32[5,768]{1,0:T(8,128)}) %tuple.101, (pred[]{:T(512)}, s32[]{:T(128)}, ...), branch_computations={%region_1.1_spmd, %region_2.16_spmd} | conditional | flops 625999872 | bytes 22551692 | solution.py:181
  137.5 2.1 multiply_reduce_fusion
  139.6 1.9 multiply_reduce_fusion.5
  145.0 4.1 %bitcast_add_fusion = f32[768,768]{1,0:T(8,128)} fusion(f32[768,768]{1,0:T(8,128)} %get-tuple-element.418, bf16[2,8,4,4,768]{4,1,3,2,0:T(8,128)(2,1)S(1)} %get-tuple-element.504, f32[2,8,4,4,768]{4,1,3,2,0:T(8,128)S(1)} %multiply_add_fusion.1, f32[768]{0:T(1024)S(1)} %get-tuple-element.471, f32[768]{0:T(1024)S(1)} %get-tuple-element.472, ...), kind=kOutput, calls=%fused_computation.25 | convolution fusion | flops 305332224 | bytes 5913600 | tf_op jit(solution)/shard_map/while/body/eval_jaxpr/cond/branch_1_fun/dot_general | solution.py:132
  150.4 9.6 %collective-permute-done = bf16[2,8,4,4,768]{4,1,3,2,0:T(8,128)(2,1)S(1)} collective-permute-done((bf16[2,8,4,4,768]{4,1,3,2,0:T(8,128)(2,1)S(1)}, bf16[2,8,4,4,768]{4,1,3,2,0:T(8,128)(2,1)S(1)}, u32[]{:S(2)}, u32[]{:S(2)}) %collective-permute-start) | collective-permute-done | bytes 393248 | tf_op jit(solution)/shard_map/while/body/eval_jaxpr/ppermute | solution.py:15
  160.0 14.6 %conditional.2 = (bf16[2,8,4,4,768]{4,1,3,2,0:T(8,128)(2,1)S(1)}, f32[768,768]{1,0:T(8,128)}, f32[9,768]{1,0:T(8,128)}, f32[5,768]{1,0:T(8,128)}) conditional(s32[]{:T(128)} %convert_element_type.67, (f32[768,768]{1,0:T(8,128)}, f32[9,768]{1,0:T(8,128)}, f32[5,768]{1,0:T(8,128)}) %tuple.101, (pred[]{:T(512)}, s32[]{:T(128)}, ...), branch_computations={%region_1.1_spmd, %region_2.16_spmd} | conditional | flops 625999872 | bytes 22551692 | solution.py:181
  162.9 2.1 multiply_reduce_fusion
  170.4 4.1 %bitcast_add_fusion = f32[768,768]{1,0:T(8,128)} fusion(f32[768,768]{1,0:T(8,128)} %get-tuple-element.418, bf16[2,8,4,4,768]{4,1,3,2,0:T(8,128)(2,1)S(1)} %get-tuple-element.504, f32[2,8,4,4,768]{4,1,3,2,0:T(8,128)S(1)} %multiply_add_fusion.1, f32[768]{0:T(1024)S(1)} %get-tuple-element.471, f32[768]{0:T(1024)S(1)} %get-tuple-element.472, ...), kind=kOutput, calls=%fused_computation.25 | convolution fusion | flops 305332224 | bytes 5913600 | tf_op jit(solution)/shard_map/while/body/eval_jaxpr/cond/branch_1_fun/dot_general | solution.py:132
  175.8 8.6 %collective-permute-done = bf16[2,8,4,4,768]{4,1,3,2,0:T(8,128)(2,1)S(1)} collective-permute-done((bf16[2,8,4,4,768]{4,1,3,2,0:T(8,128)(2,1)S(1)}, bf16[2,8,4,4,768]{4,1,3,2,0:T(8,128)(2,1)S(1)}, u32[]{:S(2)}, u32[]{:S(2)}) %collective-permute-start) | collective-permute-done | bytes 393248 | tf_op jit(solution)/shard_map/while/body/eval_jaxpr/ppermute | solution.py:15
  184.5 59.6 %all-reduce.4 = (f32[9,768]{1,0:T(8,128)S(1)}, f32[5,768]{1,0:T(8,128)S(1)}) all-reduce(f32[9,768]{1,0:T(8,128)} %get-tuple-element.445, f32[5,768]{1,0:T(8,128)} %get-tuple-element.446), channel_id=1, replica_groups=mesh['dp'=16,'section'=2] {'dp'}, use_global_device_ids=true, to_apply=%region_19.20 | all-reduce | flops 10752 | bytes 86016 | tf_op jit(solution)/shard_map/psum | solution.py:195
  (131 shorter events, 46.3 us)
Async XLA Ops:
  7.2 6.6 %copy-start = (bf16[4,128,768]{2,1,0:T(8,128)(2,1)S(1)}, bf16[4,128,768]{2,1,0:T(8,128)(2,1)}, u32[]{:S(2)}) copy-start(bf16[4,128,768]{2,1,0:T(8,128)(2,1)} %param.17) | copy-start | bytes 2359300
  7.2 44.2 %all-gather.3.cloned.1.call-start = ((), (), s32[]{:S(2)}) async-start(), calls=%async_computation.2 | async-start | bytes 1253376 | tf_op jit(solution)/shard_map/all_gather | solution.py:156
  7.9 238.1 %reduce-scatter.2.cloned.1.call-start = ((), (), s32[]{:S(2)}) async-start(), calls=%async_computation.1 | async-start | bytes 2506752 | tf_op jit(solution)/shard_map/reduce_scatter | solution.py:194
  10.7 3.1 %copy-start.3 = (s32[8]{0:T(128)S(1)}, s32[8]{0:T(128)}, u32[]{:S(2)}) copy-start(s32[8]{0:T(128)} %param.13) | copy-start | bytes 100
  13.8 1.0 copy-start.2
  54.2 26.8 %collective-permute-start = (bf16[2,8,4,4,768]{4,1,3,2,0:T(8,128)(2,1)S(1)}, bf16[2,8,4,4,768]{4,1,3,2,0:T(8,128)(2,1)S(1)}, u32[]{:S(2)}, u32[]{:S(2)}) collective-permute-start(bf16[2,8,4,4,768]{4,1,3,2,0:T(8,128)(2,1)S(1)} %get-tuple-element.591), channel_id=1, source_target_pairs={{1,0},{3,2},{5,4},{7,6},{9,8},{11,10},{13,12},{15,14},{17,16},{19,... | collective-permute-start | bytes 1179656 | tf_op jit(solution)/shard_map/while/body/eval_jaxpr/ppermute | solution.py:15
  81.0 2.9 %copy-start.1 = (bf16[768,768]{1,0:T(8,128)(2,1)S(1)}, bf16[768,768]{1,0:T(8,128)(2,1)}, u32[]{:S(2)}) copy-start(bf16[768,768]{1,0:T(8,128)(2,1)} %get-tuple-element.416) | copy-start | bytes 3538948 | tf_op jit(solution)/shard_map/while/body/eval_jaxpr/cond
  95.6 12.7 %collective-permute-start = (bf16[2,8,4,4,768]{4,1,3,2,0:T(8,128)(2,1)S(1)}, bf16[2,8,4,4,768]{4,1,3,2,0:T(8,128)(2,1)S(1)}, u32[]{:S(2)}, u32[]{:S(2)}) collective-permute-start(bf16[2,8,4,4,768]{4,1,3,2,0:T(8,128)(2,1)S(1)} %get-tuple-element.591), channel_id=1, source_target_pairs={{1,0},{3,2},{5,4},{7,6},{9,8},{11,10},{13,12},{15,14},{17,16},{19,... | collective-permute-start | bytes 1179656 | tf_op jit(solution)/shard_map/while/body/eval_jaxpr/ppermute | solution.py:15
  108.2 2.9 %copy-start.1 = (bf16[768,768]{1,0:T(8,128)(2,1)S(1)}, bf16[768,768]{1,0:T(8,128)(2,1)}, u32[]{:S(2)}) copy-start(bf16[768,768]{1,0:T(8,128)(2,1)} %get-tuple-element.416) | copy-start | bytes 3538948 | tf_op jit(solution)/shard_map/while/body/eval_jaxpr/cond
  122.8 11.8 %collective-permute-start = (bf16[2,8,4,4,768]{4,1,3,2,0:T(8,128)(2,1)S(1)}, bf16[2,8,4,4,768]{4,1,3,2,0:T(8,128)(2,1)S(1)}, u32[]{:S(2)}, u32[]{:S(2)}) collective-permute-start(bf16[2,8,4,4,768]{4,1,3,2,0:T(8,128)(2,1)S(1)} %get-tuple-element.591), channel_id=1, source_target_pairs={{1,0},{3,2},{5,4},{7,6},{9,8},{11,10},{13,12},{15,14},{17,16},{19,... | collective-permute-start | bytes 1179656 | tf_op jit(solution)/shard_map/while/body/eval_jaxpr/ppermute | solution.py:15
  134.6 2.9 %copy-start.1 = (bf16[768,768]{1,0:T(8,128)(2,1)S(1)}, bf16[768,768]{1,0:T(8,128)(2,1)}, u32[]{:S(2)}) copy-start(bf16[768,768]{1,0:T(8,128)(2,1)} %get-tuple-element.416) | copy-start | bytes 3538948 | tf_op jit(solution)/shard_map/while/body/eval_jaxpr/cond
  149.1 10.9 %collective-permute-start = (bf16[2,8,4,4,768]{4,1,3,2,0:T(8,128)(2,1)S(1)}, bf16[2,8,4,4,768]{4,1,3,2,0:T(8,128)(2,1)S(1)}, u32[]{:S(2)}, u32[]{:S(2)}) collective-permute-start(bf16[2,8,4,4,768]{4,1,3,2,0:T(8,128)(2,1)S(1)} %get-tuple-element.591), channel_id=1, source_target_pairs={{1,0},{3,2},{5,4},{7,6},{9,8},{11,10},{13,12},{15,14},{17,16},{19,... | collective-permute-start | bytes 1179656 | tf_op jit(solution)/shard_map/while/body/eval_jaxpr/ppermute | solution.py:15
  160.0 2.9 %copy-start.1 = (bf16[768,768]{1,0:T(8,128)(2,1)S(1)}, bf16[768,768]{1,0:T(8,128)(2,1)}, u32[]{:S(2)}) copy-start(bf16[768,768]{1,0:T(8,128)(2,1)} %get-tuple-element.416) | copy-start | bytes 3538948 | tf_op jit(solution)/shard_map/while/body/eval_jaxpr/cond
  174.5 9.9 %collective-permute-start = (bf16[2,8,4,4,768]{4,1,3,2,0:T(8,128)(2,1)S(1)}, bf16[2,8,4,4,768]{4,1,3,2,0:T(8,128)(2,1)S(1)}, u32[]{:S(2)}, u32[]{:S(2)}) collective-permute-start(bf16[2,8,4,4,768]{4,1,3,2,0:T(8,128)(2,1)S(1)} %get-tuple-element.591), channel_id=1, source_target_pairs={{1,0},{3,2},{5,4},{7,6},{9,8},{11,10},{13,12},{15,14},{17,16},{19,... | collective-permute-start | bytes 1179656 | tf_op jit(solution)/shard_map/while/body/eval_jaxpr/ppermute | solution.py:15
Sparse Core Ops, SparseCore 0:
  10.3 41.0 all-gather.2
  184.6 61.4 reduce-scatter.1
where the time goes:
time: 256 us; the launch traced here: 254 us
  waiting for transfers between devices  102 us (40%)
  blocking collectives  59.6 us (23%)
  other arithmetic  28.9 us (11%)
  matrix products  26.5 us (10%)
  local copies, waits for them, and re-layouts  16.4 us (6%)
  between operations  14.1 us (6%)
  starting transfers between devices  6.49 us (3%)
    ppermute x5, waiting for transfers between devices, from_behind(): return lax.ppermute(block, axis, route)  65.5 us
    psum x1, blocking collectives, local(): s_total, t_total = lax.psum((finals[2], finals[3]), 'dp')  59.6 us
    all_gather x1, waiting for transfers between devices, local(): full_weight = lax.all_gather(weight_shard, 'dp', axis=0, tiled=True)  34.8 us
    dot_general x4, matrix products, section_back(): jnp.dot(flat_hidden.T, flat_grad, preferred_element_type=jnp.float32)  16.4 us
    add x8, other arithmetic, live_work(): return (in_grad, sums[0] + w_part, sums[1] + s_part, sums[2] + t_part)  11.1 us
    dot_general x4, matrix products, hidden_of(): return jnp.dot(flat_grad, full_weight.T, preferred_element_type=jnp.float32)  8.29 us
    reduce_sum x4, other arithmetic, spatial_kernel_grad(): jnp.sum(padded[..., row_off:row_off + height, col_off:col_off + width, :]...  7.66 us
    ppermute x5, starting transfers between devices, from_behind(): return lax.ppermute(block, axis, route)  6.41 us
  transfers between devices with their start and end apart: 7, of which 7 were waited for; matrix products, arithmetic and copies ran while one was open for 4% of the time, Pallas kernels for 0%

commit v1 on v0

--- a/solution.py
+++ b/solution.py
@@ -1,12 +1,16 @@
+import functools
 import math
 
 import jax
 import jax.numpy as jnp
 from jax import lax
+from jax.experimental import pallas as pl
+from jax.experimental.pallas import tpu as pltpu
 from jax.sharding import PartitionSpec as P
 
 INV_ROOT_TWO = 0.7071067811865476
 INV_ROOT_TAU = 0.3989422804014327
+LANES = 128
 
 
 def from_behind(block, axis, distance):
@@ -135,7 +139,7 @@
     return (in_grad, weight_grad, s_part, t_part)
 
 
-def local(
+def pipelined(
     section_inputs, cotangent, sessions, point_weight, spatial_kernel, temporal_kernel, readout
 ):
     section_count = lax.axis_size("section")
@@ -200,9 +204,230 @@
     return ((weight_grads * factor)[None], (s_total * factor)[None], (t_total * factor)[None])
 
 
+def section_kernel(
+    first, frames, side, sess_ref, x_ref, g_in_ref, read_ref, w_ref, sk_ref, tk_ref, *rest
+):
+    if first:
+        ing_ref, wg_ref, st_ref, g_ref, hg_ref, hid_ref, acc_ref = rest
+    else:
+        wg_ref, st_ref, hg_ref, hid_ref, acc_ref = rest
+        g_ref = g_in_ref
+    cells = side * side
+    clip_rows = cells * frames
+    taps = tk_ref.shape[0]
+    channels = w_ref.shape[1]
+    rows = x_ref.shape[0]
+    clips = rows // clip_rows
+    if first:
+        for clip in range(clips):
+            span = pl.ds(clip * clip_rows, clip_rows)
+            g_ref[span, :] = jnp.dot(
+                g_in_ref[span, :], read_ref[sess_ref[clip]], preferred_element_type=jnp.float32
+            ).astype(jnp.bfloat16)
+    hg_ref[...] = lax.dot_general(
+        g_ref[...], w_ref[...], (((1,), (1,)), ((), ())), preferred_element_type=jnp.float32
+    )
+    acc_ref[...] = jnp.zeros_like(acc_ref)
+    frame_of = lax.broadcasted_iota(jnp.int32, (frames, LANES), 0)
+    chunks = channels // LANES
+
+    def step(index, carry):
+        clip = index // chunks
+        lanes = pl.ds(pl.multiple_of((index % chunks) * LANES, LANES), LANES)
+        span = pl.ds(pl.multiple_of(clip * clip_rows, clip_rows), clip_rows)
+
+        def tile(value):
+            return jnp.broadcast_to(value, (frames, LANES))
+
+        s_taps = [tile(sk_ref[k : k + 1, lanes]) for k in range(9)]
+        t_taps = [tile(tk_ref[d : d + 1, lanes]) for d in range(taps)]
+        t_front = [jnp.where(frame_of >= d, t_taps[d], 0.0) for d in range(taps)]
+        t_tail = [jnp.where(frame_of < frames - d, t_taps[d], 0.0) for d in range(taps)]
+        x_all = x_ref[span, lanes].astype(jnp.float32)
+        hg_all = hg_ref[span, lanes]
+        x = [x_all[c * frames : (c + 1) * frames] for c in range(cells)]
+        inside = lambda i, j: 0 <= i < side and 0 <= j < side
+        spread, sgrad, hidden = [], [], []
+        t_sums = [None] * taps
+        for i in range(side):
+            for j in range(side):
+                total = None
+                for r in range(3):
+                    for q in range(3):
+                        if inside(i + r - 1, j + q - 1):
+                            term = s_taps[3 * r + q] * x[(i + r - 1) * side + j + q - 1]
+                            total = term if total is None else total + term
+                pre = t_taps[0] * total
+                for d in range(1, taps):
+                    pre = pre + t_front[d] * pltpu.roll(total, d, 0)
+                half = 0.5 + 0.5 * lax.erf(pre * INV_ROOT_TWO)
+                hidden.append(pre * half)
+                slope = half + pre * jnp.exp(-0.5 * pre * pre) * INV_ROOT_TAU
+                c = i * side + j
+                pgrad = hg_all[c * frames : (c + 1) * frames] * slope
+                back = t_taps[0] * pgrad
+                for d in range(taps):
+                    moved = pgrad if d == 0 else pltpu.roll(pgrad, frames - d, 0)
+                    if d:
+                        back = back + t_tail[d] * moved
+                    part = total * moved
+                    t_sums[d] = part if t_sums[d] is None else t_sums[d] + part
+                sgrad.append(back)
+        hid_ref[span, lanes] = jnp.concatenate(hidden, axis=0).astype(jnp.bfloat16)
+        for d in range(taps):
+            acc_ref[9 + d, :, lanes] += t_sums[d]
+        s_sums = [None] * 9
+        for i in range(side):
+            for j in range(side):
+                for r in range(3):
+                    for q in range(3):
+                        if inside(i + r - 1, j + q - 1):
+                            part = x[(i + r - 1) * side + j + q - 1] * sgrad[i * side + j]
+                            k = 3 * r + q
+                            s_sums[k] = part if s_sums[k] is None else s_sums[k] + part
+        for k in range(9):
+            acc_ref[k, :, lanes] += s_sums[k]
+        if first:
+            out = []
+            for i in range(side):
+                for j in range(side):
+                    total = None
+                    for r in range(3):
+                        for q in range(3):
+                            if inside(i - r + 1, j - q + 1):
+                                term = s_taps[3 * r + q] * sgrad[(i - r + 1) * side + j - q + 1]
+                                total = term if total is None else total + term
+                    out.append(total)
+            ing_ref[span, lanes] = (
+                g_ref[span, lanes].astype(jnp.float32) + jnp.concatenate(out, axis=0)
+            ).astype(jnp.bfloat16)
+        return carry
+
+    lax.fori_loop(0, clips * chunks, step, 0)
+    wg_ref[...] = lax.dot_general(
+        hid_ref[...], g_ref[...], (((0,), (0,)), ((), ())), preferred_element_type=jnp.float32
+    ).astype(wg_ref.dtype)
+    wide = lax.broadcasted_iota(jnp.int32, (frames, channels), 0)
+    for k in range(9):
+        st_ref[k : k + 1, :] = jnp.sum(acc_ref[k], axis=0, keepdims=True)
+    for d in range(taps):
+        kept = jnp.where(wide < frames - d, acc_ref[9 + d], 0.0)
+        st_ref[9 + d : 10 + d, :] = jnp.sum(kept, axis=0, keepdims=True)
+
+
+def section_call(first, frames, side, sess, x, g_in, read, weight, sk, tk):
+    rows, channels = x.shape
+    vmem = pl.BlockSpec(memory_space=pltpu.VMEM)
+    out_shape = [
+        jax.ShapeDtypeStruct((channels, channels), jnp.bfloat16),
+        jax.ShapeDtypeStruct((9 + tk.shape[0], channels), jnp.float32),
+    ]
+    scratch = [
+        pltpu.VMEM((rows, channels), jnp.float32),
+        pltpu.VMEM((rows, channels), jnp.bfloat16),
+        pltpu.VMEM((9 + tk.shape[0], frames, channels), jnp.float32),
+    ]
+    if first:
+        out_shape = [jax.ShapeDtypeStruct((rows, channels), jnp.bfloat16)] + out_shape
+        scratch = [pltpu.VMEM((rows, channels), jnp.bfloat16)] + scratch
+    return pl.pallas_call(
+        functools.partial(section_kernel, first, frames, side),
+        out_shape=out_shape,
+        in_specs=[pl.BlockSpec(memory_space=pltpu.SMEM)] + [vmem] * 6,
+        out_specs=[vmem] * len(out_shape),
+        scratch_shapes=scratch,
+        compiler_params=pltpu.CompilerParams(vmem_limit_bytes=40 << 20),
+        cost_estimate=pl.CostEstimate(
+            flops=4 * rows * channels * channels, bytes_accessed=8 << 20, transcendentals=0
+        ),
+        name="section_first" if first else "section_next",
+    )(sess, x, g_in, read, weight, sk, tk)
+
+
+def dp_swap(block, mask):
+    return lax.ppermute(block, "dp", [(i, i ^ mask) for i in range(16)])
+
+
+def section_swap(block):
+    return lax.ppermute(block, "section", [(0, 1), (1, 0)])
+
+
+def pick(block, index, axis):
+    return lax.dynamic_index_in_dim(block, index, axis, keepdims=False)
+
+
+def local(
+    section_inputs, cotangent, sessions, point_weight, spatial_kernel, temporal_kernel, readout
+):
+    mine = lax.axis_index("section")
+    dp_index = lax.axis_index("dp")
+    _, clip_count, frames, side, _, channels = section_inputs.shape
+    cells = side * side
+    part = clip_count // 2
+    f32 = jnp.float32
+
+    def by_cell(block):
+        last = block.shape[-1]
+        return block.reshape(-1, frames, cells, last).transpose(0, 2, 1, 3).reshape(-1, last)
+
+    away = lax.dynamic_slice_in_dim(section_inputs[0], (1 - mine) * part, part, 0)
+    kept = lax.dynamic_slice_in_dim(section_inputs[0], mine * part, part, 0)
+    came = section_swap(by_cell(away))
+    kept = by_cell(kept)
+    x_top = jnp.where(mine == 1, kept, came)
+    x_low = jnp.where(mine == 1, came, kept)
+    cot = by_cell(lax.dynamic_slice_in_dim(cotangent, mine * part, part, 0))
+    sess = lax.dynamic_slice_in_dim(sessions, mine * part, part, 0)
+    weights = lax.all_gather(point_weight[0], ("section", "dp"), axis=0, tiled=True)
+    w_low, w_top = weights[:channels], weights[channels:]
+    kernels = jnp.concatenate([spatial_kernel[0], temporal_kernel[0]], axis=0)
+    kernels_other = section_swap(kernels)
+    k_top = jnp.where(mine == 1, kernels, kernels_other)
+    k_low = jnp.where(mine == 1, kernels_other, kernels)
+
+    in_grad, wg_top, st_top = section_call(
+        True, frames, side, sess, x_top, cot, readout, w_top, k_top[:9], k_top[9:]
+    )
+    wg_low, st_low = section_call(
+        False, frames, side, sess, x_low, in_grad, readout, w_low, k_low[:9], k_low[9:]
+    )
+
+    core = dp_index % 2
+    x_at = (dp_index // 2) % 2
+    z_at = dp_index // 4
+    bf16 = jnp.bfloat16
+
+    def core_stage(wg):
+        split = wg.reshape(4, 2, 2, channels // 16, channels)
+        got = dp_swap(pick(split, 1 - core, 2), 1)
+        return pick(split, core, 2).astype(f32) + got.astype(f32)
+
+    top_sum = core_stage(wg_top)
+    low_sum = core_stage(wg_low)
+    stacked_send = jnp.where(mine == 1, low_sum, top_sum).astype(bf16)
+    own = jnp.where(mine == 1, top_sum, low_sum)
+    own = own + section_swap(stacked_send).astype(f32)
+    got = dp_swap(pick(own, 1 - x_at, 1).astype(bf16), 2)
+    own = pick(own, x_at, 1) + got.astype(f32)
+    total = pick(own, z_at, 0)
+    narrow = own.astype(bf16)
+    for hop in range(1, 4):
+        route = [(i, (i + 4 * hop) % 16) for i in range(16)]
+        total = total + lax.ppermute(pick(narrow, (z_at + hop) % 4, 0), "dp", route).astype(f32)
+
+    st_send = jnp.where(mine == 1, st_low, st_top)
+    st_own = jnp.where(mine == 1, st_top, st_low) + section_swap(st_send)
+    for mask in (1, 2, 4, 8):
+        st_own = st_own + dp_swap(st_own, mask)
+    factor = 1.0 / math.sqrt(clip_count * lax.axis_size("dp") * frames * cells)
+    st_own = st_own * factor
+    return ((total * factor)[None], st_own[:9][None], st_own[9:][None])
+
+
 def solution(mesh):
+    halves = mesh.shape["section"] == 2 and mesh.shape["dp"] == 16
     return jax.shard_map(
-        local,
+        local if halves else pipelined,
         mesh=mesh,
         in_specs=(
             P("section", "dp", None, None, None, None),

time: 256 us -> 148 us (0.58)
  blocking collectives: 59.6 us -> 0 us
  matrix products: 26.5 us -> 0 us
  other arithmetic: 28.9 us -> 6.11 us
  Pallas kernels: 0 us -> 14.7 us
  waiting for transfers between devices: 102 us -> 88.6 us
  starting transfers between devices: 6.49 us -> 14.6 us
  local copies, waits for them, and re-layouts: 16.4 us -> 9.8 us
    psum x1 -> x0, blocking collectives: 59.6 us -> none  [local(): s_total, t_total = lax.psum((finals[2], finals[3]), 'dp')]
    dot_general x9 -> x0, matrix products: 26.5 us -> none  [the longest x4 16.4 us: section_back(): jnp.dot(flat_hidden.T, flat_grad, preferred_element_type=jnp.float32)]
    pallas_call x0 -> x2, Pallas kernels: none -> 14.7 us  [section_call(): pl.pallas_call(functools.partial(section_kernel, first, frames, side), ou...]
    ppermute x5 -> x14, waiting for transfers between devices: 65.5 us -> 51.6 us  [the longest x4 32 us: section_swap(): return lax.ppermute(block, 'section', [(0, 1), (1, 0)])]
    add x12 -> x5, other arithmetic: 12.6 us -> 1.62 us  [the longest x1 1.59 us: local(): own = own + section_swap(stacked_send).astype(f32)]
    ppermute x5 -> x14, starting transfers between devices: 6.41 us -> 14.6 us  [the longest x4 5.51 us: section_swap(): return lax.ppermute(block, 'section', [(0, 1), (1, 0)])]
    reduce_sum x4 -> x0, other arithmetic: 7.66 us -> none  [spatial_kernel_grad(): jnp.sum(padded[..., row_off:row_off + height, col_off:col_off + width, :]...]
    convert_element_type x8 -> x2, other arithmetic: 7.08 us -> 2.26 us  [the longest x1 2.19 us: local(): stacked_send = jnp.where(mine == 1, low_sum, top_sum).astype(bf16)]
  transfers between devices with their start and end apart: 7 -> 15, of which waited for: 7 -> 13; matrix products, arithmetic and copies ran while one was open for 4% -> 6% of each run, Pallas kernels for 0% -> 0%
where the time goes in v1:
time: 148 us
  waiting for transfers between devices  88.6 us (60%)
  Pallas kernels  14.7 us (10%)
  starting transfers between devices  14.6 us (10%)
  between operations  14.3 us (10%)
  local copies, waits for them, and re-layouts  9.8 us (7%)
  other arithmetic  6.11 us (4%)
    all_gather x1, waiting for transfers between devices, local(): lax.all_gather(point_weight[0], ('section', 'dp'), axis=0, tiled=True)  36.3 us
    ppermute x4, waiting for transfers between devices, section_swap(): return lax.ppermute(block, 'section', [(0, 1), (1, 0)])  32 us
    ppermute x7, waiting for transfers between devices, dp_swap(): return lax.ppermute(block, 'dp', [(i, i ^ mask) for i in range(16)])  15.5 us
    pallas_call x2, Pallas kernels, section_call(): pl.pallas_call(functools.partial(section_kernel, first, frames, side), ou...  14.7 us
    ppermute x4, starting transfers between devices, section_swap(): return lax.ppermute(block, 'section', [(0, 1), (1, 0)])  5.51 us
    ppermute x7, starting transfers between devices, dp_swap(): return lax.ppermute(block, 'dp', [(i, i ^ mask) for i in range(16)])  4.85 us
    ppermute x3, starting transfers between devices, local(): lax.ppermute(pick(narrow, (z_at + hop) % 4, 0), 'dp', route).astype(f32)  4.25 us
    ppermute x3, waiting for transfers between devices, local(): lax.ppermute(pick(narrow, (z_at + hop) % 4, 0), 'dp', route).astype(f32)  4.07 us
  transfers between devices with their start and end apart: 15, of which 13 were waited for; matrix products, arithmetic and copies ran while one was open for 6% of the time, Pallas kernels for 0%

profile of v1, /device:TPU:0, one launch (start us, length us, event | category | flops | bytes accessed | tf_op | source)
XLA Modules:
  0.0 148.1 jit_solution(17000524919282547453)
XLA Ops:
  7.9 2.0 %constant_dynamic-slice_fusion.2 = (bf16[1,4,8,4,4,768]{5,4,3,2,1,0:T(4,128)(2,1)S(1)}, bf16[1,4,8,4,4,768]{5,4,3,2,1,0:T(4,128)(2,1)S(1)}) fusion(bf16[1,8,8,4,4,768]{5,4,3,2,1,0:T(4,128)(2,1)} %param.7, s32[]{:T(128)S(6)} %select_n.113, s32[]{:T(128)S(6)} %select_n.115), kind=kLoop, calls=%fused_computation.33 | loop fusion | bytes 3145736 | tf_op jit(solution)/shard_map/dynamic_slice | solution.py:374
  10.2 3.0 %collective-permute-start = (bf16[512,768]{1,0:T(8,128)(2,1)S(1)}, bf16[512,768]{1,0:T(8,128)(2,1)}, u32[]{:S(2)}, u32[]{:S(2)}) collective-permute-start(bf16[512,768]{1,0:T(8,128)(2,1)S(1)} %bitcast.81), channel_id=1, source_target_pairs={{0,1},{1,0},{2,3},{3,2},{4,5},{5,4},{6,7},{7,6},{8,9},{9,8},{10,11... | collective-permute-start | bytes 2359304 | tf_op jit(solution)/shard_map/ppermute | solution.py:352
  14.0 1.1 copy.21
  15.1 17.3 %collective-permute-done.1 = f32[14,768]{1,0:T(8,128)S(1)} collective-permute-done((f32[14,768]{1,0:T(8,128)S(1)}, f32[14,768]{1,0:T(8,128)S(1)}, u32[]{:S(2)}, u32[]{:S(2)}) %collective-permute-start.1) | collective-permute-done | bytes 43040 | tf_op jit(solution)/shard_map/ppermute | solution.py:352
  33.0 1.5 bitcast_select_fusion
  34.5 36.3 %all-gather.3.cloned.1.call-done = bf16[1,1536,768]{2,1,0:T(8,128)(2,1)} async-done(((bf16[1,48,768]{2,1,0:T(8,128)(2,1)}), bf16[1,1536,768]{2,1,0:T(8,128)(2,1)}) %all-gather.3.cloned.1.call-update) | async-done | bytes 2359312 | tf_op jit(solution)/shard_map/all_gather | solution.py:381
  70.8 1.9 %slice_bitcast_fusion = (bf16[768,768]{1,0:T(8,128)(2,1)S(1)}, bf16[768,768]{1,0:T(8,128)(2,1)S(1)}) fusion(bf16[1,1536,768]{2,1,0:T(8,128)(2,1)} %all-gather.3.cloned.1.call-done), kind=kLoop, calls=%fused_computation | loop fusion | bytes 4718592 | tf_op jit(solution)/shard_map/slice | solution.py:382
  72.7 7.8 %section_first.1 = (bf16[512,768]{1,0:T(8,128)(2,1)S(1)}, bf16[768,768]{1,0:T(8,128)(2,1)S(1)}, f32[14,768]{1,0:T(8,128)S(1)}) custom-call(s32[4]{0:T(128)S(1)} %dynamic_slice.46.sess_ref, bf16[512,768]{1,0:T(8,128)(2,1)S(1)} %get-tuple-element.24.x_ref, bf16[512,128]{1,0:T(8,128)(2,1)S(1)} %bitcast.78, bf16[4,128,768]{2,1,0:T(8,128)(2,1)S(1)} %copy-done.2, ...), custom_call_target="tpu_custom_call" | custom-call | flops 1207959552 | bytes 8388608 | tf_op jit(solution)/shard_map/section_first/pallas_call | solution.py:333
  81.2 6.9 %section_next.1 = (bf16[768,768]{1,0:T(8,128)(2,1)S(1)}, f32[14,768]{1,0:T(8,128)S(1)}) custom-call(s32[4]{0:T(128)S(1)} %copy-done.4, bf16[512,768]{1,0:T(8,128)(2,1)S(1)} %get-tuple-element.23.x_ref, bf16[512,768]{1,0:T(8,128)(2,1)S(1)} %get-tuple-element.9.g_in_ref, bf16[4,128,768]{2,1,0:T(8,128)(2,1)S(1)} %copy-done.2, ...), custom_call_target="tpu_custom_call" | custom-call | flops 1207959552 | bytes 8388608 | tf_op jit(solution)/shard_map/section_next/pallas_call | solution.py:333
  90.3 1.7 %collective-permute-done.2 = bf16[4,2,48,768]{3,2,1,0:T(8,128)(2,1)S(1)} collective-permute-done((bf16[4,2,48,768]{3,2,1,0:T(8,128)(2,1)}, bf16[4,2,48,768]{3,2,1,0:T(8,128)(2,1)S(1)}, u32[]{:S(2)}, u32[]{:S(2)}) %collective-permute-start.2) | collective-permute-done | bytes 589856 | tf_op jit(solution)/shard_map/ppermute | solution.py:348
  93.0 2.2 %select_convert_fusion = bf16[4,2,48,768]{3,2,1,0:T(8,128)(2,1)} fusion(bf16[4,2,48,768]{3,2,1,0:T(8,128)(2,1)S(1)} %collective-permute-done.2, bf16[4,2,48,768]{3,2,1,0:T(8,128)(2,1)} %collective-permute-done.3, pred[]{:T(512)S(6)} %eq.8, bf16[4,2,2,48,768]{4,3,2,1,0:T(8,128)(2,1)S(1)} %bitcast.76, s32[]{:T(128)S(6)} %select_n.120, ...), kind=kLoop, calls=%fused_computation.5 | loop fusion | flops 2359296 | bytes 2949125 | tf_op jit(solution)/shard_map/convert_element_type | solution.py:407
  95.2 1.5 collective-permute-start.4
  97.2 14.7 %collective-permute-done.9 = f32[14,768]{1,0:T(8,128)S(1)} collective-permute-done((f32[14,768]{1,0:T(8,128)S(1)}, f32[14,768]{1,0:T(8,128)S(1)}, u32[]{:S(2)}, u32[]{:S(2)}) %collective-permute-start.9) | collective-permute-done | bytes 43040 | tf_op jit(solution)/shard_map/ppermute | solution.py:352
  112.1 1.2 collective-permute-done.10
  113.3 1.5 %collective-permute-start.11 = (f32[14,768]{1,0:T(8,128)S(1)}, f32[14,768]{1,0:T(8,128)S(1)}, u32[]{:S(2)}, u32[]{:S(2)}) collective-permute-start(f32[14,768]{1,0:T(8,128)S(1)} %add.129), channel_id=1, source_target_pairs={{0,4},{2,6},{4,0},{6,2},{8,12},{10,14},{12,8},{14,10},{16,20},{18,... | collective-permute-start | bytes 129032 | tf_op jit(solution)/shard_map/ppermute | solution.py:348
  114.8 2.7 %collective-permute-done.11 = f32[14,768]{1,0:T(8,128)S(1)} collective-permute-done((f32[14,768]{1,0:T(8,128)S(1)}, f32[14,768]{1,0:T(8,128)S(1)}, u32[]{:S(2)}, u32[]{:S(2)}) %collective-permute-start.11) | collective-permute-done | bytes 43040 | tf_op jit(solution)/shard_map/ppermute | solution.py:348
  117.9 3.7 %collective-permute-done.12 = f32[14,768]{1,0:T(8,128)S(1)} collective-permute-done((f32[14,768]{1,0:T(8,128)S(1)}, f32[14,768]{1,0:T(8,128)S(1)}, u32[]{:S(2)}, u32[]{:S(2)}) %collective-permute-start.12) | collective-permute-done | bytes 43040 | tf_op jit(solution)/shard_map/ppermute | solution.py:348
  122.4 1.6 %convert_add_fusion.2 = f32[4,2,48,768]{3,2,1,0:T(8,128)S(1)} fusion(bf16[4,2,48,768]{3,2,1,0:T(8,128)(2,1)} %collective-permute-done.4, bf16[4,2,48,768]{3,2,1,0:T(8,128)(2,1)S(1)} %collective-permute-done.2, bf16[4,2,48,768]{3,2,1,0:T(8,128)(2,1)} %collective-permute-done.3, pred[]{:T(512)S(6)} %eq.8, bf16[4,2,2,48,768]{4,3,2,1,0:T(8,128)(2,1)S(1)} %bitcast.77, ...), kind=kLoop, calls=%fused_computation.4 | loop fusion | flops 2654208 | bytes 4128773 | tf_op jit(solution)/shard_map/add | solution.py:409
  124.1 1.5 %collective-permute-start.5 = (bf16[4,48,768]{2,1,0:T(8,128)(2,1)S(1)}, bf16[4,48,768]{2,1,0:T(8,128)(2,1)S(1)}, u32[]{:S(2)}, u32[]{:S(2)}) collective-permute-start(bf16[4,48,768]{2,1,0:T(8,128)(2,1)S(1)} %fusion), channel_id=1, source_target_pairs={{0,4},{2,6},{4,0},{6,2},{8,12},{10,14},{12,8},{14,10},{16,20},{18,... | collective-permute-start | bytes 884744 | tf_op jit(solution)/shard_map/ppermute | solution.py:348
  125.5 1.5 %collective-permute-done.13 = f32[14,768]{1,0:T(8,128)S(1)} collective-permute-done((f32[14,768]{1,0:T(8,128)S(1)}, f32[14,768]{1,0:T(8,128)S(1)}, u32[]{:S(2)}, u32[]{:S(2)}) %collective-permute-start.13) | collective-permute-done | bytes 43040 | tf_op jit(solution)/shard_map/ppermute | solution.py:348
  127.1 3.8 %collective-permute-done.5 = bf16[4,48,768]{2,1,0:T(8,128)(2,1)S(1)} collective-permute-done((bf16[4,48,768]{2,1,0:T(8,128)(2,1)S(1)}, bf16[4,48,768]{2,1,0:T(8,128)(2,1)S(1)}, u32[]{:S(2)}, u32[]{:S(2)}) %collective-permute-start.5) | collective-permute-done | bytes 294944 | tf_op jit(solution)/shard_map/ppermute | solution.py:348
  131.0 2.1 %collective-permute-start.6 = (bf16[48,768]{1,0:T(8,128)(2,1)S(1)}, bf16[48,768]{1,0:T(8,128)(2,1)S(1)}, u32[]{:S(2)}, u32[]{:S(2)}) collective-permute-start(bf16[48,768]{1,0:T(8,128)(2,1)S(1)} %get-tuple-element.27), channel_id=1, source_target_pairs={{0,8},{2,10},{4,12},{6,14},{8,16},{10,18},{12,20},{14,22},{16,24},... | collective-permute-start | bytes 221192 | tf_op jit(solution)/shard_map/ppermute | solution.py:416
  133.0 1.8 %collective-permute-start.8 = (bf16[48,768]{1,0:T(8,128)(2,1)S(1)}, bf16[48,768]{1,0:T(8,128)(2,1)S(1)}, u32[]{:S(2)}, u32[]{:S(2)}) collective-permute-start(bf16[48,768]{1,0:T(8,128)(2,1)S(1)} %get-tuple-element.28), channel_id=1, source_target_pairs={{0,24},{2,26},{4,28},{6,30},{8,0},{10,2},{12,4},{14,6},{16,8},{18,... | collective-permute-start | bytes 221192 | tf_op jit(solution)/shard_map/ppermute | solution.py:416
  137.9 2.6 %collective-permute-done.7 = bf16[48,768]{1,0:T(8,128)(2,1)S(1)} collective-permute-done((bf16[48,768]{1,0:T(8,128)(2,1)S(1)}, bf16[48,768]{1,0:T(8,128)(2,1)S(1)}, u32[]{:S(2)}, u32[]{:S(2)}) %collective-permute-start.7) | collective-permute-done | bytes 73760 | tf_op jit(solution)/shard_map/ppermute | solution.py:416
  (57 shorter events, 12.1 us)
Async XLA Ops:
  7.2 6.6 %copy-start = (bf16[8,8,4,4,128]{4,3,2,1,0:T(4,128)(2,1)S(1)}, bf16[8,8,4,4,128]{4,3,2,1,0:T(4,128)(2,1)}, u32[]{:S(2)}) copy-start(bf16[8,8,4,4,128]{4,3,2,1,0:T(4,128)(2,1)} %param.8) | copy-start | bytes 786436
  7.2 63.6 %all-gather.3.cloned.1.call-start = ((), (), s32[]{:S(2)}) async-start(), calls=%async_computation | async-start | bytes 2433024 | tf_op jit(solution)/shard_map/all_gather | solution.py:381
  9.9 3.3 %copy-start.6 = (f32[1,5,768]{2,0,1:T(1,128)S(1)}, f32[1,5,768]{2,0,1:T(1,128)}, u32[]{:S(2)}) copy-start(f32[1,5,768]{2,0,1:T(1,128)} %param.12) | copy-start | bytes 46084
  9.9 3.3 %copy-start.5 = (f32[1,9,768]{2,0,1:T(1,128)S(1)}, f32[1,9,768]{2,0,1:T(1,128)}, u32[]{:S(2)}) copy-start(f32[1,9,768]{2,0,1:T(1,128)} %param.11) | copy-start | bytes 82948
  10.0 3.9 %copy-start.7 = (s32[8]{0:T(128)S(1)}, s32[8]{0:T(128)}, u32[]{:S(2)}) copy-start(s32[8]{0:T(128)} %param.9) | copy-start | bytes 100
  10.2 22.8 %collective-permute-start = (bf16[512,768]{1,0:T(8,128)(2,1)S(1)}, bf16[512,768]{1,0:T(8,128)(2,1)}, u32[]{:S(2)}, u32[]{:S(2)}) collective-permute-start(bf16[512,768]{1,0:T(8,128)(2,1)S(1)} %bitcast.81), channel_id=1, source_target_pairs={{0,1},{1,0},{2,3},{3,2},{4,5},{5,4},{6,7},{7,6},{8,9},{9,8},{10,11... | collective-permute-start | bytes 2359304 | tf_op jit(solution)/shard_map/ppermute | solution.py:352
  13.3 19.1 %collective-permute-start.1 = (f32[14,768]{1,0:T(8,128)S(1)}, f32[14,768]{1,0:T(8,128)S(1)}, u32[]{:S(2)}, u32[]{:S(2)}) collective-permute-start(f32[14,768]{1,0:T(8,128)S(1)} %pad_maximum_fusion), channel_id=1, source_target_pairs={{0,1},{1,0},{2,3},{3,2},{4,5},{5,4},{6,7},{7,6},{8,9},{9,8},{10,11... | collective-permute-start | bytes 129032 | tf_op jit(solution)/shard_map/ppermute | solution.py:352
  13.9 58.8 %copy-start.3 = (s32[4]{0:T(128)}, s32[4]{0:T(128)S(1)}, u32[]{:S(2)}) copy-start(s32[4]{0:T(128)S(1)} %dynamic_slice.46.sess_ref) | copy-start | bytes 52
  70.8 1.9 %copy-start.2 = (bf16[4,128,768]{2,1,0:T(8,128)(2,1)S(1)}, bf16[4,128,768]{2,1,0:T(8,128)(2,1)}, u32[]{:S(2)}) copy-start(bf16[4,128,768]{2,1,0:T(8,128)(2,1)} %read_ref.3) | copy-start | bytes 2359300
  72.7 7.8 %copy-start.1 = (f32[5,768]{1,0:T(8,128)S(1)}, f32[5,768]{1,0:T(8,128)}, u32[]{:S(2)}) copy-start(f32[5,768]{1,0:T(8,128)} %slice.39.tk_ref) | copy-start | bytes 46084
  80.5 0.7 copy-start.4
  89.8 2.2 %collective-permute-start.2 = (bf16[4,2,48,768]{3,2,1,0:T(8,128)(2,1)}, bf16[4,2,48,768]{3,2,1,0:T(8,128)(2,1)S(1)}, u32[]{:S(2)}, u32[]{:S(2)}) collective-permute-start(bf16[4,2,48,768]{3,2,1,0:T(8,128)(2,1)} %dynamic-slice_bitcast_fusion.1), channel_id=1, source_target_pairs={{0,2},{2,0},{4,6},{6,4},{8,10},{10,8},{12,14},{14,12},{16,18},{18,... | collective-permute-start | bytes 1769480 | tf_op jit(solution)/shard_map/ppermute | solution.py:348
  90.1 2.9 %collective-permute-start.3 = (bf16[4,2,48,768]{3,2,1,0:T(8,128)(2,1)}, bf16[4,2,48,768]{3,2,1,0:T(8,128)(2,1)}, u32[]{:S(2)}, u32[]{:S(2)}) collective-permute-start(bf16[4,2,48,768]{3,2,1,0:T(8,128)(2,1)} %dynamic-slice_bitcast_fusion), channel_id=1, source_target_pairs={{0,2},{2,0},{4,6},{6,4},{8,10},{10,8},{12,14},{14,12},{16,18},{18,... | collective-permute-start | bytes 1769480 | tf_op jit(solution)/shard_map/ppermute | solution.py:348
  95.2 27.2 %collective-permute-start.4 = (bf16[4,2,48,768]{3,2,1,0:T(8,128)(2,1)}, bf16[4,2,48,768]{3,2,1,0:T(8,128)(2,1)}, u32[]{:S(2)}, u32[]{:S(2)}) collective-permute-start(bf16[4,2,48,768]{3,2,1,0:T(8,128)(2,1)} %select_convert_fusion), channel_id=1, source_target_pairs={{0,1},{1,0},{2,3},{3,2},{4,5},{5,4},{6,7},{7,6},{8,9},{9,8},{10,11... | collective-permute-start | bytes 1769480 | tf_op jit(solution)/shard_map/ppermute | solution.py:352
  96.7 15.3 %collective-permute-start.9 = (f32[14,768]{1,0:T(8,128)S(1)}, f32[14,768]{1,0:T(8,128)S(1)}, u32[]{:S(2)}, u32[]{:S(2)}) collective-permute-start(f32[14,768]{1,0:T(8,128)S(1)} %broadcast_select_fusion), channel_id=1, source_target_pairs={{0,1},{1,0},{2,3},{3,2},{4,5},{5,4},{6,7},{7,6},{8,9},{9,8},{10,11... | collective-permute-start | bytes 129032 | tf_op jit(solution)/shard_map/ppermute | solution.py:352
  112.0 1.3 collective-permute-start.10
  113.3 4.2 %collective-permute-start.11 = (f32[14,768]{1,0:T(8,128)S(1)}, f32[14,768]{1,0:T(8,128)S(1)}, u32[]{:S(2)}, u32[]{:S(2)}) collective-permute-start(f32[14,768]{1,0:T(8,128)S(1)} %add.129), channel_id=1, source_target_pairs={{0,4},{2,6},{4,0},{6,2},{8,12},{10,14},{12,8},{14,10},{16,20},{18,... | collective-permute-start | bytes 129032 | tf_op jit(solution)/shard_map/ppermute | solution.py:348
  117.4 4.1 %collective-permute-start.12 = (f32[14,768]{1,0:T(8,128)S(1)}, f32[14,768]{1,0:T(8,128)S(1)}, u32[]{:S(2)}, u32[]{:S(2)}) collective-permute-start(f32[14,768]{1,0:T(8,128)S(1)} %add.130), channel_id=1, source_target_pairs={{0,8},{2,10},{4,12},{6,14},{8,0},{10,2},{12,4},{14,6},{16,24},{18,... | collective-permute-start | bytes 129032 | tf_op jit(solution)/shard_map/ppermute | solution.py:348
  121.6 5.4 %collective-permute-start.13 = (f32[14,768]{1,0:T(8,128)S(1)}, f32[14,768]{1,0:T(8,128)S(1)}, u32[]{:S(2)}, u32[]{:S(2)}) collective-permute-start(f32[14,768]{1,0:T(8,128)S(1)} %add.131), channel_id=1, source_target_pairs={{0,16},{2,18},{4,20},{6,22},{8,24},{10,26},{12,28},{14,30},{16,0},... | collective-permute-start | bytes 129032 | tf_op jit(solution)/shard_map/ppermute | solution.py:348
  124.1 6.8 %collective-permute-start.5 = (bf16[4,48,768]{2,1,0:T(8,128)(2,1)S(1)}, bf16[4,48,768]{2,1,0:T(8,128)(2,1)S(1)}, u32[]{:S(2)}, u32[]{:S(2)}) collective-permute-start(bf16[4,48,768]{2,1,0:T(8,128)(2,1)S(1)} %fusion), channel_id=1, source_target_pairs={{0,4},{2,6},{4,0},{6,2},{8,12},{10,14},{12,8},{14,10},{16,20},{18,... | collective-permute-start | bytes 884744 | tf_op jit(solution)/shard_map/ppermute | solution.py:348
  131.0 6.3 %collective-permute-start.6 = (bf16[48,768]{1,0:T(8,128)(2,1)S(1)}, bf16[48,768]{1,0:T(8,128)(2,1)S(1)}, u32[]{:S(2)}, u32[]{:S(2)}) collective-permute-start(bf16[48,768]{1,0:T(8,128)(2,1)S(1)} %get-tuple-element.27), channel_id=1, source_target_pairs={{0,8},{2,10},{4,12},{6,14},{8,16},{10,18},{12,20},{14,22},{16,24},... | collective-permute-start | bytes 221192 | tf_op jit(solution)/shard_map/ppermute | solution.py:416
  133.0 4.9 %collective-permute-start.8 = (bf16[48,768]{1,0:T(8,128)(2,1)S(1)}, bf16[48,768]{1,0:T(8,128)(2,1)S(1)}, u32[]{:S(2)}, u32[]{:S(2)}) collective-permute-start(bf16[48,768]{1,0:T(8,128)(2,1)S(1)} %get-tuple-element.28), channel_id=1, source_target_pairs={{0,24},{2,26},{4,28},{6,30},{8,0},{10,2},{12,4},{14,6},{16,8},{18,... | collective-permute-start | bytes 221192 | tf_op jit(solution)/shard_map/ppermute | solution.py:416
  134.8 5.7 %collective-permute-start.7 = (bf16[48,768]{1,0:T(8,128)(2,1)S(1)}, bf16[48,768]{1,0:T(8,128)(2,1)S(1)}, u32[]{:S(2)}, u32[]{:S(2)}) collective-permute-start(bf16[48,768]{1,0:T(8,128)(2,1)S(1)} %get-tuple-element.29), channel_id=1, source_target_pairs={{0,16},{2,18},{4,20},{6,22},{8,24},{10,26},{12,28},{14,30},{16,0},... | collective-permute-start | bytes 221192 | tf_op jit(solution)/shard_map/ppermute | solution.py:416
Sparse Core Ops, SparseCore 0:
  10.9 59.8 all-gather.2

commit v2 on v1

--- a/solution.py
+++ b/solution.py
@@ -11,6 +11,7 @@
 INV_ROOT_TWO = 0.7071067811865476
 INV_ROOT_TAU = 0.3989422804014327
 LANES = 128
+MESH = pl.DeviceIdType.MESH
 
 
 def from_behind(block, axis, distance):
@@ -204,17 +205,12 @@
     return ((weight_grads * factor)[None], (s_total * factor)[None], (t_total * factor)[None])
 
 
-def section_kernel(
-    first, frames, side, sess_ref, x_ref, g_in_ref, read_ref, w_ref, sk_ref, tk_ref, *rest
+def section_work(
+    first, frames, side, sess_ref, x_ref, g_in_ref, read_ref, w_ref, k_ref, taps, wg_ref, st_ref,
+    ing_ref, g_ref, hg_ref, hid_ref, acc_ref
 ):
-    if first:
-        ing_ref, wg_ref, st_ref, g_ref, hg_ref, hid_ref, acc_ref = rest
-    else:
-        wg_ref, st_ref, hg_ref, hid_ref, acc_ref = rest
-        g_ref = g_in_ref
     cells = side * side
     clip_rows = cells * frames
-    taps = tk_ref.shape[0]
     channels = w_ref.shape[1]
     rows = x_ref.shape[0]
     clips = rows // clip_rows
@@ -239,8 +235,8 @@
         def tile(value):
             return jnp.broadcast_to(value, (frames, LANES))
 
-        s_taps = [tile(sk_ref[k : k + 1, lanes]) for k in range(9)]
-        t_taps = [tile(tk_ref[d : d + 1, lanes]) for d in range(taps)]
+        s_taps = [tile(k_ref[k : k + 1, lanes]) for k in range(9)]
+        t_taps = [tile(k_ref[9 + d : 10 + d, lanes]) for d in range(taps)]
         t_front = [jnp.where(frame_of >= d, t_taps[d], 0.0) for d in range(taps)]
         t_tail = [jnp.where(frame_of < frames - d, t_taps[d], 0.0) for d in range(taps)]
         x_all = x_ref[span, lanes].astype(jnp.float32)
@@ -308,6 +304,7 @@
         hid_ref[...], g_ref[...], (((0,), (0,)), ((), ())), preferred_element_type=jnp.float32
     ).astype(wg_ref.dtype)
     wide = lax.broadcasted_iota(jnp.int32, (frames, channels), 0)
+    st_ref[...] = jnp.zeros_like(st_ref)
     for k in range(9):
         st_ref[k : k + 1, :] = jnp.sum(acc_ref[k], axis=0, keepdims=True)
     for d in range(taps):
@@ -315,52 +312,284 @@
         st_ref[9 + d : 10 + d, :] = jnp.sum(kept, axis=0, keepdims=True)
 
 
-def section_call(first, frames, side, sess, x, g_in, read, weight, sk, tk):
-    rows, channels = x.shape
+def both_kernel(
+    frames, side, taps, sess_ref, x_ref, cot_ref, read_ref, w_ref, k_ref, wg_ref, st_ref, *scratch
+):
+    ing_ref, g_ref, hg_ref, hid_ref, acc_ref = scratch
+    for sec in (1, 0):
+        section_work(
+            sec == 1,
+            frames,
+            side,
+            sess_ref,
+            x_ref.at[sec],
+            cot_ref,
+            read_ref,
+            w_ref.at[sec],
+            k_ref.at[sec],
+            taps,
+            wg_ref.at[sec],
+            st_ref.at[sec],
+            ing_ref,
+            g_ref if sec == 1 else ing_ref,
+            hg_ref,
+            hid_ref,
+            acc_ref,
+        )
+
+
+def both_call(frames, side, taps, sess, x, cot, read, weights, kernels):
+    _, rows, channels = x.shape
     vmem = pl.BlockSpec(memory_space=pltpu.VMEM)
-    out_shape = [
-        jax.ShapeDtypeStruct((channels, channels), jnp.bfloat16),
-        jax.ShapeDtypeStruct((9 + tk.shape[0], channels), jnp.float32),
+    return pl.pallas_call(
+        functools.partial(both_kernel, frames, side, taps),
+        out_shape=[
+            jax.ShapeDtypeStruct((2, channels, channels), jnp.bfloat16),
+            jax.ShapeDtypeStruct((2, 16, channels), jnp.float32),
+        ],
+        in_specs=[pl.BlockSpec(memory_space=pltpu.SMEM)] + [vmem] * 5,
+        out_specs=[vmem] * 2,
+        scratch_shapes=[
+            pltpu.VMEM((rows, channels), jnp.bfloat16),
+            pltpu.VMEM((rows, channels), jnp.bfloat16),
+            pltpu.VMEM((rows, channels), jnp.float32),
+            pltpu.VMEM((rows, channels), jnp.bfloat16),
+            pltpu.VMEM((9 + taps, frames, channels), jnp.float32),
+        ],
+        compiler_params=pltpu.CompilerParams(vmem_limit_bytes=40 << 20),
+        name="both_sections",
+    )(sess, x, cot, read, weights, kernels)
+
+
+def places():
+    dp = lax.axis_index("dp")
+    sec = lax.axis_index("section")
+    return dp, sec, dp // 4, (dp // 2) % 2, dp % 2
+
+
+def greet(partners):
+    barrier = pltpu.get_barrier_semaphore()
+    for there in partners:
+        pl.semaphore_signal(barrier, inc=1, device_id=there, device_id_type=MESH)
+    pl.semaphore_wait(barrier, len(partners))
+
+
+def remote(src, dst, sems, slot, there):
+    return pltpu.make_async_remote_copy(
+        src_ref=src,
+        dst_ref=dst,
+        send_sem=sems[0].at[slot],
+        recv_sem=sems[1].at[slot],
+        device_id=there,
+        device_id_type=MESH,
+    )
+
+
+def gather_kernel(
+    x_ref, w_ref, k_ref, xo_ref, wo_ref, ko_ref, ys, yr, zs, zr, xs, xr, cs, cr, own_sem
+):
+    dp, sec, z, x, c = places()
+    over = (dp, 1 - sec)
+    mate = (z * 4 + x * 2 + 1 - c, sec)
+    side_chip = (z * 4 + (1 - x) * 2 + c, sec)
+    line = [((z + h) % 4 * 4 + x * 2 + c, sec) for h in (1, 2, 3)]
+    greet([over, mate, side_chip] + line)
+    secs = (sec, 1 - sec)
+    sends = []
+
+    def go(src, dst, sems, slot, there):
+        copy = remote(src, dst, sems, slot, there)
+        copy.start()
+        sends.append(copy)
+        return copy
+
+    slot_of = wo_ref.at[sec, dp]
+    y_w = go(w_ref, slot_of, (ys, yr), 0, over)
+    y_k = go(k_ref, ko_ref.at[sec], (ys, yr), 1, over)
+    y_x = go(x_ref.at[1 - sec], xo_ref.at[sec], (ys, yr), 2, over)
+    z_w = {}
+    x_w = {}
+    c_w = {}
+    for h in range(3):
+        z_w[0, h] = go(w_ref, slot_of, (zs, zr), h, line[h])
+    x_w[0, 0] = go(w_ref, slot_of, (xs, xr), 0, side_chip)
+    c_w[0, 0] = go(w_ref, slot_of, (cs, cr), 0, mate)
+    kept = [
+        pltpu.make_async_copy(w_ref, slot_of, own_sem.at[0]),
+        pltpu.make_async_copy(k_ref, ko_ref.at[sec], own_sem.at[1]),
+        pltpu.make_async_copy(x_ref.at[sec], xo_ref.at[sec], own_sem.at[2]),
     ]
-    scratch = [
-        pltpu.VMEM((rows, channels), jnp.float32),
-        pltpu.VMEM((rows, channels), jnp.bfloat16),
-        pltpu.VMEM((9 + tk.shape[0], frames, channels), jnp.float32),
-    ]
-    if first:
-        out_shape = [jax.ShapeDtypeStruct((rows, channels), jnp.bfloat16)] + out_shape
-        scratch = [pltpu.VMEM((rows, channels), jnp.bfloat16)] + scratch
+    for copy in kept:
+        copy.start()
+    y_w.wait_recv()
+    held = wo_ref.at[1 - sec, dp]
+    for h in range(3):
+        z_w[1, h] = go(held, held, (zs, zr), 3 + h, line[h])
+    x_w[1, 0] = go(held, held, (xs, xr), 4, side_chip)
+    c_w[1, 0] = go(held, held, (cs, cr), 8, mate)
+    for h in range(3):
+        source = (z + 3 - h) % 4 * 4 + x * 2 + c
+        for kind in range(2):
+            z_w[kind, h].wait_recv()
+            held = wo_ref.at[secs[kind], source]
+            x_w[kind, h + 1] = go(held, held, (xs, xr), 4 * kind + h + 1, side_chip)
+            c_w[kind, h + 1] = go(held, held, (cs, cr), 8 * kind + h + 1, mate)
+    for h in range(4):
+        source = (z + 4 - h) % 4 * 4 + (1 - x) * 2 + c
+        for kind in range(2):
+            x_w[kind, h].wait_recv()
+            held = wo_ref.at[secs[kind], source]
+            c_w[kind, h + 4] = go(held, held, (cs, cr), 8 * kind + h + 4, mate)
+    for copy in c_w.values():
+        copy.wait_recv()
+    y_k.wait_recv()
+    y_x.wait_recv()
+    for copy in sends:
+        copy.wait_send()
+    for copy in kept:
+        copy.wait()
+
+
+def gather_call(x, w, k):
+    vmem = pl.BlockSpec(memory_space=pltpu.VMEM)
+    any_space = pl.BlockSpec(memory_space=pl.ANY)
+    dma = pltpu.SemaphoreType.DMA
     return pl.pallas_call(
-        functools.partial(section_kernel, first, frames, side),
-        out_shape=out_shape,
-        in_specs=[pl.BlockSpec(memory_space=pltpu.SMEM)] + [vmem] * 6,
-        out_specs=[vmem] * len(out_shape),
-        scratch_shapes=scratch,
-        compiler_params=pltpu.CompilerParams(vmem_limit_bytes=40 << 20),
-        cost_estimate=pl.CostEstimate(
-            flops=4 * rows * channels * channels, bytes_accessed=8 << 20, transcendentals=0
-        ),
-        name="section_first" if first else "section_next",
-    )(sess, x, g_in, read, weight, sk, tk)
-
-
-def dp_swap(block, mask):
-    return lax.ppermute(block, "dp", [(i, i ^ mask) for i in range(16)])
-
-
-def section_swap(block):
-    return lax.ppermute(block, "section", [(0, 1), (1, 0)])
-
-
-def pick(block, index, axis):
-    return lax.dynamic_index_in_dim(block, index, axis, keepdims=False)
+        gather_kernel,
+        out_shape=[
+            jax.ShapeDtypeStruct(x.shape, x.dtype),
+            jax.ShapeDtypeStruct((2, 16) + w.shape, w.dtype),
+            jax.ShapeDtypeStruct((2,) + k.shape, k.dtype),
+        ],
+        in_specs=[vmem] * 3,
+        out_specs=[any_space] * 3,
+        scratch_shapes=[dma((n,)) for n in (3, 3, 6, 6, 8, 8, 16, 16, 3)],
+        compiler_params=pltpu.CompilerParams(collective_id=0, has_side_effects=True),
+        name="gather_weights",
+    )(x, w, k)
+
+
+def reduce_kernel(factor, wg_ref, st_ref, out_ref, sto_ref, *scratch):
+    cgot, ysend, ygot, acc, xsend, xgot, zsend, zgot, ssend, sgot = scratch[:10]
+    cs, cr, ys, yr, xs, xr, zs, zr, ss, sr = scratch[10:]
+    dp, sec, z, x, c = places()
+    over = (dp, 1 - sec)
+    mate = (z * 4 + x * 2 + 1 - c, sec)
+    side_chip = (z * 4 + (1 - x) * 2 + c, sec)
+    line = [((z + h) % 4 * 4 + x * 2 + c, sec) for h in (1, 2, 3)]
+    greet([over, mate, side_chip] + line)
+    f32 = jnp.float32
+    secs = (1 - sec, sec)
+    block = [(z + 1 + k) % 4 for k in range(4)]
+    sends = []
+
+    def go(src, dst, sems, slot, there):
+        copy = remote(src, dst, sems, slot, there)
+        copy.start()
+        sends.append(copy)
+        return copy
+
+    core = {}
+    for kind in range(2):
+        for k in range(4):
+            core[kind, k] = go(
+                wg_ref.at[secs[kind], block[k], :, 1 - c],
+                cgot.at[kind, k],
+                (cs, cr),
+                4 * kind + k,
+                mate,
+            )
+    small = [go(st_ref.at[1 - sec], sgot.at[0], (ss, sr), 0, over)]
+    small_to = [mate, side_chip, (dp + 4 - 8 * (z % 2), sec), ((dp + 8) % 16, sec)]
+
+    def small_step(n):
+        small[n].wait_recv()
+        value = (st_ref[sec] if n == 0 else ssend[n - 1]) + sgot[n]
+        if n == 4:
+            sto_ref[...] = value * factor
+        else:
+            ssend[n] = value
+            small.append(go(ssend.at[n], sgot.at[n + 1], (ss, sr), n + 1, small_to[n]))
+
+    y_c = []
+    for k in range(4):
+        core[0, k].wait_recv()
+        for h in range(2):
+            ysend[k, h] = (
+                wg_ref[1 - sec, block[k], h, c].astype(f32) + cgot[0, k, h].astype(f32)
+            ).astype(jnp.bfloat16)
+        y_c.append(go(ysend.at[k], ygot.at[k], (ys, yr), k, over))
+    x_c = []
+    z_c = []
+    for k in range(5):
+        if k < 4:
+            core[1, k].wait_recv()
+            y_c[k].wait_recv()
+
+            def summed(h):
+                return (
+                    wg_ref[sec, block[k], h, c].astype(f32)
+                    + cgot[1, k, h].astype(f32)
+                    + ygot[k, h].astype(f32)
+                )
+
+            xsend[k] = summed(1 - x).astype(jnp.bfloat16)
+            x_c.append(go(xsend.at[k], xgot.at[k], (xs, xr), k, side_chip))
+            acc[k] = summed(x)
+        if k > 0:
+            x_c[k - 1].wait_recv()
+            value = acc[k - 1] + xgot[k - 1].astype(f32)
+            if k < 4:
+                zsend[k - 1] = value.astype(jnp.bfloat16)
+                z_c.append(go(zsend.at[k - 1], zgot.at[k - 1], (zs, zr), k - 1, line[k - 1]))
+            else:
+                acc[3] = value
+        small_step(k)
+    total = acc[3]
+    for k in range(3):
+        z_c[k].wait_recv()
+        total = total + zgot[k].astype(f32)
+    out_ref[...] = total * factor
+    for copy in sends:
+        copy.wait_send()
+
+
+def reduce_call(factor, wg, st):
+    _, channels, _ = wg.shape
+    depth = channels // 16
+    vmem = pl.BlockSpec(memory_space=pltpu.VMEM)
+    dma = pltpu.SemaphoreType.DMA
+    bf16, f32 = jnp.bfloat16, jnp.float32
+    return pl.pallas_call(
+        functools.partial(reduce_kernel, factor),
+        out_shape=[
+            jax.ShapeDtypeStruct((depth, channels), f32),
+            jax.ShapeDtypeStruct(st.shape[1:], f32),
+        ],
+        in_specs=[vmem] * 2,
+        out_specs=[vmem] * 2,
+        scratch_shapes=[
+            pltpu.VMEM((2, 4, 2, depth, channels), bf16),
+            pltpu.VMEM((4, 2, depth, channels), bf16),
+            pltpu.VMEM((4, 2, depth, channels), bf16),
+            pltpu.VMEM((4, depth, channels), f32),
+            pltpu.VMEM((4, depth, channels), bf16),
+            pltpu.VMEM((4, depth, channels), bf16),
+            pltpu.VMEM((3, depth, channels), bf16),
+            pltpu.VMEM((3, depth, channels), bf16),
+            pltpu.VMEM((4,) + st.shape[1:], f32),
+            pltpu.VMEM((5,) + st.shape[1:], f32),
+        ]
+        + [dma((n,)) for n in (8, 8, 4, 4, 4, 4, 3, 3, 5, 5)],
+        compiler_params=pltpu.CompilerParams(collective_id=1, has_side_effects=True),
+        name="reduce_grads",
+    )(wg.reshape(2, 4, 2, 2, depth, channels), st)
 
 
 def local(
     section_inputs, cotangent, sessions, point_weight, spatial_kernel, temporal_kernel, readout
 ):
     mine = lax.axis_index("section")
-    dp_index = lax.axis_index("dp")
     _, clip_count, frames, side, _, channels = section_inputs.shape
     cells = side * side
     part = clip_count // 2
@@ -370,58 +599,19 @@
         last = block.shape[-1]
         return block.reshape(-1, frames, cells, last).transpose(0, 2, 1, 3).reshape(-1, last)
 
-    away = lax.dynamic_slice_in_dim(section_inputs[0], (1 - mine) * part, part, 0)
-    kept = lax.dynamic_slice_in_dim(section_inputs[0], mine * part, part, 0)
-    came = section_swap(by_cell(away))
-    kept = by_cell(kept)
-    x_top = jnp.where(mine == 1, kept, came)
-    x_low = jnp.where(mine == 1, came, kept)
+    taps = temporal_kernel.shape[1]
+    halves = by_cell(section_inputs[0]).reshape(2, -1, channels)
     cot = by_cell(lax.dynamic_slice_in_dim(cotangent, mine * part, part, 0))
     sess = lax.dynamic_slice_in_dim(sessions, mine * part, part, 0)
-    weights = lax.all_gather(point_weight[0], ("section", "dp"), axis=0, tiled=True)
-    w_low, w_top = weights[:channels], weights[channels:]
-    kernels = jnp.concatenate([spatial_kernel[0], temporal_kernel[0]], axis=0)
-    kernels_other = section_swap(kernels)
-    k_top = jnp.where(mine == 1, kernels, kernels_other)
-    k_low = jnp.where(mine == 1, kernels_other, kernels)
-
-    in_grad, wg_top, st_top = section_call(
-        True, frames, side, sess, x_top, cot, readout, w_top, k_top[:9], k_top[9:]
-    )
-    wg_low, st_low = section_call(
-        False, frames, side, sess, x_low, in_grad, readout, w_low, k_low[:9], k_low[9:]
-    )
-
-    core = dp_index % 2
-    x_at = (dp_index // 2) % 2
-    z_at = dp_index // 4
-    bf16 = jnp.bfloat16
-
-    def core_stage(wg):
-        split = wg.reshape(4, 2, 2, channels // 16, channels)
-        got = dp_swap(pick(split, 1 - core, 2), 1)
-        return pick(split, core, 2).astype(f32) + got.astype(f32)
-
-    top_sum = core_stage(wg_top)
-    low_sum = core_stage(wg_low)
-    stacked_send = jnp.where(mine == 1, low_sum, top_sum).astype(bf16)
-    own = jnp.where(mine == 1, top_sum, low_sum)
-    own = own + section_swap(stacked_send).astype(f32)
-    got = dp_swap(pick(own, 1 - x_at, 1).astype(bf16), 2)
-    own = pick(own, x_at, 1) + got.astype(f32)
-    total = pick(own, z_at, 0)
-    narrow = own.astype(bf16)
-    for hop in range(1, 4):
-        route = [(i, (i + 4 * hop) % 16) for i in range(16)]
-        total = total + lax.ppermute(pick(narrow, (z_at + hop) % 4, 0), "dp", route).astype(f32)
-
-    st_send = jnp.where(mine == 1, st_low, st_top)
-    st_own = jnp.where(mine == 1, st_top, st_low) + section_swap(st_send)
-    for mask in (1, 2, 4, 8):
-        st_own = st_own + dp_swap(st_own, mask)
+    spare = jnp.zeros((16 - 9 - taps, channels), f32)
+    kernels = jnp.concatenate([spatial_kernel[0], temporal_kernel[0], spare], axis=0)
+    x_both, w_both, k_both = gather_call(halves, point_weight[0], kernels)
+    wg, st = both_call(
+        frames, side, taps, sess, x_both, cot, readout, w_both.reshape(2, channels, channels), k_both
+    )
     factor = 1.0 / math.sqrt(clip_count * lax.axis_size("dp") * frames * cells)
-    st_own = st_own * factor
-    return ((total * factor)[None], st_own[:9][None], st_own[9:][None])
+    grads, small = reduce_call(factor, wg, st)
+    return (grads[None], small[:9][None], small[9 : 9 + taps][None])
 
 
 def solution(mesh):

time: 148 us -> 87 us (0.59)
  waiting for transfers between devices: 88.6 us -> 0 us
  Pallas kernels: 14.7 us -> 69.1 us
  starting transfers between devices: 14.6 us -> 0 us
  between operations: 14.3 us -> 0.71 us
  local copies, waits for them, and re-layouts: 9.8 us -> 15.9 us
  other arithmetic: 6.11 us -> 0.69 us
    pallas_call x2 -> x3, Pallas kernels: 14.7 us -> 69.1 us  [the longest x1 28.8 us: gather_call(): pl.pallas_call(gather_kernel, out_shape=[jax.ShapeDtypeStruct(x.shape, x....]
    ppermute x14 -> x0, waiting for transfers between devices: 51.6 us -> none  [the longest x4 32 us: section_swap(): return lax.ppermute(block, 'section', [(0, 1), (1, 0)])]
    all_gather x1 -> x0, waiting for transfers between devices: 36.3 us -> none  [local(): lax.all_gather(point_weight[0], ('section', 'dp'), axis=0, tiled=True)]
    ppermute x14 -> x0, starting transfers between devices: 14.6 us -> none  [the longest x4 5.51 us: section_swap(): return lax.ppermute(block, 'section', [(0, 1), (1, 0)])]
    unnamed x23 -> x20, local copies, waits for them, and re-layouts: 3.37 us -> 10.4 us
    another operation x0 -> x1, local copies, waits for them, and re-layouts: none -> 3.07 us  [by_cell(): block.reshape(-1, frames, cells, last).transpose(0, 2, 1, 3)]
    slice x3 -> x0, local copies, waits for them, and re-layouts: 2.47 us -> none  [the longest x1 1.85 us: local(): w_low, w_top = (weights[:channels], weights[channels:])]
    convert_element_type x2 -> x0, other arithmetic: 2.26 us -> none  [the longest x1 2.19 us: local(): stacked_send = jnp.where(mine == 1, low_sum, top_sum).astype(bf16)]
  transfers between devices with their start and end apart: 15 -> 0, of which waited for: 13 -> 0; matrix products, arithmetic and copies ran while one was open for 6% -> 0% of each run, Pallas kernels for 0% -> 0%
where the time goes in v2:
time: 87 us; the launch traced here: 86.4 us
  Pallas kernels  69.1 us (79%)
  local copies, waits for them, and re-layouts  15.9 us (18%)
    pallas_call x1, Pallas kernels, gather_call(): pl.pallas_call(gather_kernel, out_shape=[jax.ShapeDtypeStruct(x.shape, x....  28.8 us
    pallas_call x1, Pallas kernels, reduce_call(): pl.pallas_call(functools.partial(reduce_kernel, factor), out_shape=[jax.S...  26.9 us
    pallas_call x1, Pallas kernels, both_call(): pl.pallas_call(functools.partial(both_kernel, frames, side, taps), out_sh...  13.5 us
    unnamed x20, local copies, waits for them, and re-layouts  10.4 us
    another operation x1, local copies, waits for them, and re-layouts, by_cell(): block.reshape(-1, frames, cells, last).transpose(0, 2, 1, 3)  3.07 us

profile of v2, /device:TPU:0, one launch (start us, length us, event | category | flops | bytes accessed | tf_op | source)
XLA Modules:
  0.0 86.4 jit_solution(7807343866588670822)
XLA Ops:
  0.6 0.0 copy-start
  0.6 0.8 dynamic_slice.6.sess_ref
  1.4 0.1 pad.2.clone
  1.5 0.7 copy.24
  2.2 0.7 copy.23
  3.0 0.7 maximum_maximum_fusion.k_ref
  3.7 0.0 copy-done
  3.8 3.1 %copy.17 = bf16[1,8,8,4,4,768]{5,2,4,3,1,0:T(8,128)(2,1)} copy(bf16[1,8,8,4,4,768]{5,4,3,2,1,0:T(4,128)(2,1)} %param.7) | data formatting | bytes 3145728 | tf_op jit(solution)/shard_map/reshape;squeeze | solution.py:600
  6.8 28.8 %gather_weights.1 = (bf16[2,512,768]{2,1,0:T(8,128)(2,1)}, bf16[2,16,48,768]{3,2,1,0:T(8,128)(2,1)}, f32[2,16,768]{2,1,0:T(8,128)}) custom-call(bf16[2,512,768]{2,1,0:T(8,128)(2,1)} %bitcast.27, bf16[48,768]{1,0:T(8,128)(2,1)} %bitcast.31, f32[16,768]{1,0:T(8,128)} %maximum_maximum_fusion.k_ref), custom_call_target="tpu_custom_call" | custom-call | tf_op jit(solution)/shard_map/gather_weights/pallas_call | solution.py:457
  35.6 0.0 copy-done.4
  35.6 0.0 copy-start.1
  35.6 1.7 %copy-done.1 = bf16[2,16,48,768]{3,2,1,0:T(8,128)(2,1)S(1)} copy-done((bf16[2,16,48,768]{3,2,1,0:T(8,128)(2,1)S(1)}, bf16[2,16,48,768]{3,2,1,0:T(8,128)(2,1)}, u32[]{:S(2)}) %copy-start.1) | copy-done | bytes 2359320
  37.3 1.4 %copy-done.3 = bf16[2,512,768]{2,1,0:T(8,128)(2,1)S(1)} copy-done((bf16[2,512,768]{2,1,0:T(8,128)(2,1)S(1)}, bf16[2,512,768]{2,1,0:T(8,128)(2,1)}, u32[]{:S(2)}) %copy-start.3) | copy-done | bytes 1572888
  38.7 0.9 %copy-done.6 = f32[2,16,768]{2,1,0:T(8,128)S(1)} copy-done((f32[2,16,768]{2,1,0:T(8,128)S(1)}, f32[2,16,768]{2,1,0:T(8,128)}, u32[]{:S(2)}) %copy-start.6) | copy-done | bytes 98328
  39.6 13.5 %both_sections.1 = (bf16[2,768,768]{2,1,0:T(8,128)(2,1)S(1)}, f32[2,16,768]{2,1,0:T(8,128)S(1)}) custom-call(s32[4]{0:T(128)S(1)} %dynamic_slice.6.sess_ref, bf16[2,512,768]{2,1,0:T(8,128)(2,1)S(1)} %copy-done.3, bf16[512,128]{1,0:T(8,128)(2,1)S(1)} %bitcast.26, bf16[4,128,768]{2,1,0:T(8,128)(2,1)S(1)} %copy-done.4, bf16[2,768,768]{2,1,0:T(8,128)(2,1)S(1)} %bitcast.24, ...), custom_call_target="tpu_custom_call" | custom-call | tf_op jit(solution)/shard_map/both_sections/pallas_call | solution.py:344
  53.1 0.0 copy-start.2
  53.1 1.4 %copy-done.2 = bf16[2,768,768]{2,1,0:T(8,128)(2,1)} copy-done((bf16[2,768,768]{2,1,0:T(8,128)(2,1)}, bf16[2,768,768]{2,1,0:T(8,128)(2,1)S(1)}, u32[]{:S(2)}) %copy-start.2) | copy-done | bytes 2359320
  54.5 0.6 copy-done.5
  55.1 26.9 %reduce_grads.1 = (f32[48,768]{1,0:T(8,128)}, f32[16,768]{1,0:T(8,128)}) custom-call(bf16[2,4,2,2,48,768]{5,4,3,2,1,0:T(8,128)(2,1)} %bitcast.25, f32[2,16,768]{2,1,0:T(8,128)} %copy-done.5), custom_call_target="tpu_custom_call" | custom-call | tf_op jit(solution)/shard_map/reduce_grads/pallas_call | solution.py:563
  82.0 0.7 slice_bitcast_fusion.1
  82.8 0.6 copy.16
  83.4 0.8 slice_bitcast_fusion
  84.2 0.6 copy.15
  84.8 1.6 %copy.26 = f32[1,48,768]{2,1,0:T(8,128)} copy(f32[1,48,768]{2,1,0:T(8,128)} %bitcast.29) | data formatting | bytes 294912
  (7 shorter events, 0.1 us)
Async XLA Ops:
  0.6 3.0 %copy-start = (bf16[8,8,4,4,128]{4,3,2,1,0:T(4,128)(2,1)S(1)}, bf16[8,8,4,4,128]{4,3,2,1,0:T(4,128)(2,1)}, u32[]{:S(2)}) copy-start(bf16[8,8,4,4,128]{4,3,2,1,0:T(4,128)(2,1)} %param.8) | copy-start | bytes 786436
  6.8 28.8 %copy-start.4 = (bf16[4,128,768]{2,1,0:T(8,128)(2,1)S(1)}, bf16[4,128,768]{2,1,0:T(8,128)(2,1)}, u32[]{:S(2)}) copy-start(bf16[4,128,768]{2,1,0:T(8,128)(2,1)} %read_ref.1) | copy-start | bytes 2359300
  35.6 1.7 %copy-start.1 = (bf16[2,16,48,768]{3,2,1,0:T(8,128)(2,1)S(1)}, bf16[2,16,48,768]{3,2,1,0:T(8,128)(2,1)}, u32[]{:S(2)}) copy-start(bf16[2,16,48,768]{3,2,1,0:T(8,128)(2,1)} %get-tuple-element.11) | copy-start | bytes 7077892
  37.3 1.4 %copy-start.3 = (bf16[2,512,768]{2,1,0:T(8,128)(2,1)S(1)}, bf16[2,512,768]{2,1,0:T(8,128)(2,1)}, u32[]{:S(2)}) copy-start(bf16[2,512,768]{2,1,0:T(8,128)(2,1)} %get-tuple-element.10.x_ref) | copy-start | bytes 4718596
  38.7 0.9 %copy-start.6 = (f32[2,16,768]{2,1,0:T(8,128)S(1)}, f32[2,16,768]{2,1,0:T(8,128)}, u32[]{:S(2)}) copy-start(f32[2,16,768]{2,1,0:T(8,128)} %get-tuple-element.12.k_ref) | copy-start | bytes 294916
  53.1 1.4 %copy-start.2 = (bf16[2,768,768]{2,1,0:T(8,128)(2,1)}, bf16[2,768,768]{2,1,0:T(8,128)(2,1)S(1)}, u32[]{:S(2)}) copy-start(bf16[2,768,768]{2,1,0:T(8,128)(2,1)S(1)} %get-tuple-element.13) | copy-start | bytes 7077892
  54.5 0.6 copy-start.5

commit v3 on v2

--- a/solution.py
+++ b/solution.py
@@ -206,22 +206,25 @@
 
 
 def section_work(
-    first, frames, side, sess_ref, x_ref, g_in_ref, read_ref, w_ref, k_ref, taps, wg_ref, st_ref,
-    ing_ref, g_ref, hg_ref, hid_ref, acc_ref
+    first, frames, side, mine, sess_ref, x_ref, g_in_ref, read_ref, w_ref, sk_ref, tk_ref, wg_ref,
+    st_ref, ing_ref, g_ref, hg_ref, hid_ref, acc_ref, middle
 ):
+    taps = tk_ref.shape[0]
     cells = side * side
     clip_rows = cells * frames
-    channels = w_ref.shape[1]
+    channels = x_ref.shape[1]
     rows = x_ref.shape[0]
     clips = rows // clip_rows
     if first:
         for clip in range(clips):
             span = pl.ds(clip * clip_rows, clip_rows)
             g_ref[span, :] = jnp.dot(
-                g_in_ref[span, :], read_ref[sess_ref[clip]], preferred_element_type=jnp.float32
+                g_in_ref[mine, span, :],
+                read_ref[sess_ref[mine * clips + clip]],
+                preferred_element_type=jnp.float32,
             ).astype(jnp.bfloat16)
     hg_ref[...] = lax.dot_general(
-        g_ref[...], w_ref[...], (((1,), (1,)), ((), ())), preferred_element_type=jnp.float32
+        g_ref[...], w_ref[...].reshape(channels, channels), (((1,), (1,)), ((), ())), preferred_element_type=jnp.float32
     )
     acc_ref[...] = jnp.zeros_like(acc_ref)
     frame_of = lax.broadcasted_iota(jnp.int32, (frames, LANES), 0)
@@ -235,8 +238,8 @@
         def tile(value):
             return jnp.broadcast_to(value, (frames, LANES))
 
-        s_taps = [tile(k_ref[k : k + 1, lanes]) for k in range(9)]
-        t_taps = [tile(k_ref[9 + d : 10 + d, lanes]) for d in range(taps)]
+        s_taps = [tile(sk_ref[k, :, lanes]) for k in range(9)]
+        t_taps = [tile(tk_ref[d, :, lanes]) for d in range(taps)]
         t_front = [jnp.where(frame_of >= d, t_taps[d], 0.0) for d in range(taps)]
         t_tail = [jnp.where(frame_of < frames - d, t_taps[d], 0.0) for d in range(taps)]
         x_all = x_ref[span, lanes].astype(jnp.float32)
@@ -299,10 +302,16 @@
             ).astype(jnp.bfloat16)
         return carry
 
-    lax.fori_loop(0, clips * chunks, step, 0)
-    wg_ref[...] = lax.dot_general(
+    if middle is None:
+        lax.fori_loop(0, clips * chunks, step, 0)
+    else:
+        lax.fori_loop(0, clips * chunks // 2, step, 0)
+        middle()
+        lax.fori_loop(clips * chunks // 2, clips * chunks, step, 0)
+    wg = lax.dot_general(
         hid_ref[...], g_ref[...], (((0,), (0,)), ((), ())), preferred_element_type=jnp.float32
-    ).astype(wg_ref.dtype)
+    )
+    wg_ref[...] = wg.astype(wg_ref.dtype).reshape(wg_ref.shape)
     wide = lax.broadcasted_iota(jnp.int32, (frames, channels), 0)
     st_ref[...] = jnp.zeros_like(st_ref)
     for k in range(9):
@@ -310,55 +319,6 @@
     for d in range(taps):
         kept = jnp.where(wide < frames - d, acc_ref[9 + d], 0.0)
         st_ref[9 + d : 10 + d, :] = jnp.sum(kept, axis=0, keepdims=True)
-
-
-def both_kernel(
-    frames, side, taps, sess_ref, x_ref, cot_ref, read_ref, w_ref, k_ref, wg_ref, st_ref, *scratch
-):
-    ing_ref, g_ref, hg_ref, hid_ref, acc_ref = scratch
-    for sec in (1, 0):
-        section_work(
-            sec == 1,
-            frames,
-            side,
-            sess_ref,
-            x_ref.at[sec],
-            cot_ref,
-            read_ref,
-            w_ref.at[sec],
-            k_ref.at[sec],
-            taps,
-            wg_ref.at[sec],
-            st_ref.at[sec],
-            ing_ref,
-            g_ref if sec == 1 else ing_ref,
-            hg_ref,
-            hid_ref,
-            acc_ref,
-        )
-
-
-def both_call(frames, side, taps, sess, x, cot, read, weights, kernels):
-    _, rows, channels = x.shape
-    vmem = pl.BlockSpec(memory_space=pltpu.VMEM)
-    return pl.pallas_call(
-        functools.partial(both_kernel, frames, side, taps),
-        out_shape=[
-            jax.ShapeDtypeStruct((2, channels, channels), jnp.bfloat16),
-            jax.ShapeDtypeStruct((2, 16, channels), jnp.float32),
-        ],
-        in_specs=[pl.BlockSpec(memory_space=pltpu.SMEM)] + [vmem] * 5,
-        out_specs=[vmem] * 2,
-        scratch_shapes=[
-            pltpu.VMEM((rows, channels), jnp.bfloat16),
-            pltpu.VMEM((rows, channels), jnp.bfloat16),
-            pltpu.VMEM((rows, channels), jnp.float32),
-            pltpu.VMEM((rows, channels), jnp.bfloat16),
-            pltpu.VMEM((9 + taps, frames, channels), jnp.float32),
-        ],
-        compiler_params=pltpu.CompilerParams(vmem_limit_bytes=40 << 20),
-        name="both_sections",
-    )(sess, x, cot, read, weights, kernels)
 
 
 def places():
@@ -385,9 +345,30 @@
     )
 
 
-def gather_kernel(
-    x_ref, w_ref, k_ref, xo_ref, wo_ref, ko_ref, ys, yr, zs, zr, xs, xr, cs, cr, own_sem
+def whole_kernel(
+    frames,
+    side,
+    factor,
+    sess_ref,
+    x_ref,
+    cot_ref,
+    read_ref,
+    w_ref,
+    sk_ref,
+    tk_ref,
+    out_ref,
+    so_ref,
+    to_ref,
+    *scratch,
 ):
+    xo_ref, wo_ref, sko_ref, tko_ref, wg_ref, st_ref = scratch[:6]
+    work = scratch[6:11]
+    cgot, xsend, xgot, acc, ysend, ygot, zsend, zgot, ssend, sgot = scratch[11:21]
+    ays, ayr, azs, azr, axs, axr, acs, acr, own_sem = scratch[21:30]
+    cs, cr, xs, xr, ys, yr, zs, zr, ss, sr = scratch[30:]
+    f32, bf16 = jnp.float32, jnp.bfloat16
+    taps = tk_ref.shape[0]
+    channels = w_ref.shape[1]
     dp, sec, z, x, c = places()
     over = (dp, 1 - sec)
     mate = (z * 4 + x * 2 + 1 - c, sec)
@@ -395,6 +376,7 @@
     line = [((z + h) % 4 * 4 + x * 2 + c, sec) for h in (1, 2, 3)]
     greet([over, mate, side_chip] + line)
     secs = (sec, 1 - sec)
+    block = [(z + 1 + k) % 4 for k in range(4)]
     sends = []
 
     def go(src, dst, sems, slot, there):
@@ -404,101 +386,97 @@
         return copy
 
     slot_of = wo_ref.at[sec, dp]
-    y_w = go(w_ref, slot_of, (ys, yr), 0, over)
-    y_k = go(k_ref, ko_ref.at[sec], (ys, yr), 1, over)
-    y_x = go(x_ref.at[1 - sec], xo_ref.at[sec], (ys, yr), 2, over)
+    y_w = go(w_ref, slot_of, (ays, ayr), 0, over)
     z_w = {}
     x_w = {}
     c_w = {}
     for h in range(3):
-        z_w[0, h] = go(w_ref, slot_of, (zs, zr), h, line[h])
-    x_w[0, 0] = go(w_ref, slot_of, (xs, xr), 0, side_chip)
-    c_w[0, 0] = go(w_ref, slot_of, (cs, cr), 0, mate)
+        z_w[0, h] = go(w_ref, slot_of, (azs, azr), h, line[h])
+    x_w[0, 0] = go(w_ref, slot_of, (axs, axr), 0, side_chip)
+    c_w[0, 0] = go(w_ref, slot_of, (acs, acr), 0, mate)
+    y_rest = [
+        go(sk_ref, sko_ref.at[sec], (ays, ayr), 1, over),
+        go(tk_ref, tko_ref.at[sec], (ays, ayr), 2, over),
+        go(x_ref.at[1 - sec], xo_ref.at[sec], (ays, ayr), 3, over),
+    ]
     kept = [
         pltpu.make_async_copy(w_ref, slot_of, own_sem.at[0]),
-        pltpu.make_async_copy(k_ref, ko_ref.at[sec], own_sem.at[1]),
-        pltpu.make_async_copy(x_ref.at[sec], xo_ref.at[sec], own_sem.at[2]),
+        pltpu.make_async_copy(sk_ref, sko_ref.at[sec], own_sem.at[1]),
+        pltpu.make_async_copy(tk_ref, tko_ref.at[sec], own_sem.at[2]),
+        pltpu.make_async_copy(x_ref.at[sec], xo_ref.at[sec], own_sem.at[3]),
     ]
     for copy in kept:
         copy.start()
     y_w.wait_recv()
     held = wo_ref.at[1 - sec, dp]
     for h in range(3):
-        z_w[1, h] = go(held, held, (zs, zr), 3 + h, line[h])
-    x_w[1, 0] = go(held, held, (xs, xr), 4, side_chip)
-    c_w[1, 0] = go(held, held, (cs, cr), 8, mate)
+        z_w[1, h] = go(held, held, (azs, azr), 3 + h, line[h])
+    x_w[1, 0] = go(held, held, (axs, axr), 4, side_chip)
+    c_w[1, 0] = go(held, held, (acs, acr), 8, mate)
     for h in range(3):
         source = (z + 3 - h) % 4 * 4 + x * 2 + c
         for kind in range(2):
             z_w[kind, h].wait_recv()
             held = wo_ref.at[secs[kind], source]
-            x_w[kind, h + 1] = go(held, held, (xs, xr), 4 * kind + h + 1, side_chip)
-            c_w[kind, h + 1] = go(held, held, (cs, cr), 8 * kind + h + 1, mate)
+            x_w[kind, h + 1] = go(held, held, (axs, axr), 4 * kind + h + 1, side_chip)
+            c_w[kind, h + 1] = go(held, held, (acs, acr), 8 * kind + h + 1, mate)
     for h in range(4):
         source = (z + 4 - h) % 4 * 4 + (1 - x) * 2 + c
         for kind in range(2):
             x_w[kind, h].wait_recv()
             held = wo_ref.at[secs[kind], source]
-            c_w[kind, h + 4] = go(held, held, (cs, cr), 8 * kind + h + 4, mate)
+            c_w[kind, h + 4] = go(held, held, (acs, acr), 8 * kind + h + 4, mate)
     for copy in c_w.values():
         copy.wait_recv()
-    y_k.wait_recv()
-    y_x.wait_recv()
-    for copy in sends:
-        copy.wait_send()
+    for copy in y_rest:
+        copy.wait_recv()
     for copy in kept:
         copy.wait()
 
-
-def gather_call(x, w, k):
-    vmem = pl.BlockSpec(memory_space=pltpu.VMEM)
-    any_space = pl.BlockSpec(memory_space=pl.ANY)
-    dma = pltpu.SemaphoreType.DMA
-    return pl.pallas_call(
-        gather_kernel,
-        out_shape=[
-            jax.ShapeDtypeStruct(x.shape, x.dtype),
-            jax.ShapeDtypeStruct((2, 16) + w.shape, w.dtype),
-            jax.ShapeDtypeStruct((2,) + k.shape, k.dtype),
-        ],
-        in_specs=[vmem] * 3,
-        out_specs=[any_space] * 3,
-        scratch_shapes=[dma((n,)) for n in (3, 3, 6, 6, 8, 8, 16, 16, 3)],
-        compiler_params=pltpu.CompilerParams(collective_id=0, has_side_effects=True),
-        name="gather_weights",
-    )(x, w, k)
-
-
-def reduce_kernel(factor, wg_ref, st_ref, out_ref, sto_ref, *scratch):
-    cgot, ysend, ygot, acc, xsend, xgot, zsend, zgot, ssend, sgot = scratch[:10]
-    cs, cr, ys, yr, xs, xr, zs, zr, ss, sr = scratch[10:]
-    dp, sec, z, x, c = places()
-    over = (dp, 1 - sec)
-    mate = (z * 4 + x * 2 + 1 - c, sec)
-    side_chip = (z * 4 + (1 - x) * 2 + c, sec)
-    line = [((z + h) % 4 * 4 + x * 2 + c, sec) for h in (1, 2, 3)]
-    greet([over, mate, side_chip] + line)
-    f32 = jnp.float32
-    secs = (1 - sec, sec)
-    block = [(z + 1 + k) % 4 for k in range(4)]
-    sends = []
-
-    def go(src, dst, sems, slot, there):
-        copy = remote(src, dst, sems, slot, there)
-        copy.start()
-        sends.append(copy)
-        return copy
+    def compute(s, middle):
+        ing_ref, g_ref, hg_ref, hid_ref, acc_ref = work
+        section_work(
+            s == 1,
+            frames,
+            side,
+            sec,
+            sess_ref,
+            xo_ref.at[s],
+            cot_ref,
+            read_ref,
+            wo_ref.at[s],
+            sko_ref.at[s],
+            tko_ref.at[s],
+            wg_ref.at[s],
+            st_ref.at[s],
+            ing_ref,
+            g_ref if s == 1 else ing_ref,
+            hg_ref,
+            hid_ref,
+            acc_ref,
+            middle,
+        )
 
     core = {}
-    for kind in range(2):
+
+    def core_stage(s):
         for k in range(4):
-            core[kind, k] = go(
-                wg_ref.at[secs[kind], block[k], :, 1 - c],
-                cgot.at[kind, k],
-                (cs, cr),
-                4 * kind + k,
-                mate,
+            core[s, k] = go(
+                wg_ref.at[s, block[k], :, 1 - c], cgot.at[s, k], (cs, cr), 4 * s + k, mate
             )
+
+    def x_stage(s):
+        for k in range(4):
+            core[s, k].wait_recv()
+            xsend[s, k] = (
+                wg_ref[s, block[k], 1 - x, c].astype(f32) + cgot[s, k, 1 - x].astype(f32)
+            ).astype(bf16)
+            go(xsend.at[s, k], xgot.at[s, k], (xs, xr), 4 * s + k, side_chip)
+
+    compute(1, None)
+    core_stage(1)
+    compute(0, lambda: x_stage(1))
+    core_stage(0)
     small = [go(st_ref.at[1 - sec], sgot.at[0], (ss, sr), 0, over)]
     small_to = [mate, side_chip, (dp + 4 - 8 * (z % 2), sec), ((dp + 8) % 16, sec)]
 
@@ -506,46 +484,44 @@
         small[n].wait_recv()
         value = (st_ref[sec] if n == 0 else ssend[n - 1]) + sgot[n]
         if n == 4:
-            sto_ref[...] = value * factor
+            value = value * factor
+            for k in range(9):
+                so_ref[k] = value[k : k + 1]
+            for d in range(taps):
+                to_ref[d] = value[9 + d : 10 + d]
         else:
             ssend[n] = value
             small.append(go(ssend.at[n], sgot.at[n + 1], (ss, sr), n + 1, small_to[n]))
 
+    x_stage(0)
+
+    def chip_pair_sum(s, k):
+        remote(xsend.at[s, k], xgot.at[s, k], (xs, xr), 4 * s + k, side_chip).wait_recv()
+        return (
+            wg_ref[s, block[k], x, c].astype(f32)
+            + cgot[s, k, x].astype(f32)
+            + xgot[s, k].astype(f32)
+        )
+
     y_c = []
     for k in range(4):
-        core[0, k].wait_recv()
-        for h in range(2):
-            ysend[k, h] = (
-                wg_ref[1 - sec, block[k], h, c].astype(f32) + cgot[0, k, h].astype(f32)
-            ).astype(jnp.bfloat16)
+        ysend[k] = chip_pair_sum(1 - sec, k).astype(bf16)
         y_c.append(go(ysend.at[k], ygot.at[k], (ys, yr), k, over))
-    x_c = []
+        if k % 2:
+            small_step(k // 2)
     z_c = []
-    for k in range(5):
-        if k < 4:
-            core[1, k].wait_recv()
-            y_c[k].wait_recv()
-
-            def summed(h):
-                return (
-                    wg_ref[sec, block[k], h, c].astype(f32)
-                    + cgot[1, k, h].astype(f32)
-                    + ygot[k, h].astype(f32)
-                )
-
-            xsend[k] = summed(1 - x).astype(jnp.bfloat16)
-            x_c.append(go(xsend.at[k], xgot.at[k], (xs, xr), k, side_chip))
-            acc[k] = summed(x)
-        if k > 0:
-            x_c[k - 1].wait_recv()
-            value = acc[k - 1] + xgot[k - 1].astype(f32)
-            if k < 4:
-                zsend[k - 1] = value.astype(jnp.bfloat16)
-                z_c.append(go(zsend.at[k - 1], zgot.at[k - 1], (zs, zr), k - 1, line[k - 1]))
-            else:
-                acc[3] = value
-        small_step(k)
-    total = acc[3]
+    for k in range(4):
+        value = chip_pair_sum(sec, k)
+        y_c[k].wait_recv()
+        value = value + ygot[k].astype(f32)
+        if k < 3:
+            zsend[k] = value.astype(bf16)
+            z_c.append(go(zsend.at[k], zgot.at[k], (zs, zr), k, line[k]))
+        else:
+            acc[...] = value
+        if k < 3:
+            small_step(2 + k)
+    total = acc[...]
     for k in range(3):
         z_c[k].wait_recv()
         total = total + zgot[k].astype(f32)
@@ -554,64 +530,81 @@
         copy.wait_send()
 
 
-def reduce_call(factor, wg, st):
-    _, channels, _ = wg.shape
-    depth = channels // 16
+def whole_call(frames, side, factor, sess, x, cot, read, w, sk, tk):
+    _, rows, channels = x.shape
+    depth = w.shape[0]
+    taps = tk.shape[0]
     vmem = pl.BlockSpec(memory_space=pltpu.VMEM)
     dma = pltpu.SemaphoreType.DMA
     bf16, f32 = jnp.bfloat16, jnp.float32
+    wide = (depth, channels)
     return pl.pallas_call(
-        functools.partial(reduce_kernel, factor),
+        functools.partial(whole_kernel, frames, side, factor),
         out_shape=[
-            jax.ShapeDtypeStruct((depth, channels), f32),
-            jax.ShapeDtypeStruct(st.shape[1:], f32),
+            jax.ShapeDtypeStruct(wide, f32),
+            jax.ShapeDtypeStruct(sk.shape, f32),
+            jax.ShapeDtypeStruct(tk.shape, f32),
         ],
-        in_specs=[vmem] * 2,
-        out_specs=[vmem] * 2,
+        in_specs=[pl.BlockSpec(memory_space=pltpu.SMEM)] + [vmem] * 6,
+        out_specs=[vmem] * 3,
         scratch_shapes=[
-            pltpu.VMEM((2, 4, 2, depth, channels), bf16),
-            pltpu.VMEM((4, 2, depth, channels), bf16),
-            pltpu.VMEM((4, 2, depth, channels), bf16),
-            pltpu.VMEM((4, depth, channels), f32),
-            pltpu.VMEM((4, depth, channels), bf16),
-            pltpu.VMEM((4, depth, channels), bf16),
-            pltpu.VMEM((3, depth, channels), bf16),
-            pltpu.VMEM((3, depth, channels), bf16),
-            pltpu.VMEM((4,) + st.shape[1:], f32),
-            pltpu.VMEM((5,) + st.shape[1:], f32),
+            pltpu.VMEM(x.shape, bf16),
+            pltpu.VMEM((2, 16) + wide, bf16),
+            pltpu.VMEM((2,) + sk.shape, f32),
+            pltpu.VMEM((2,) + tk.shape, f32),
+            pltpu.VMEM((2, 4, 2, 2) + wide, bf16),
+            pltpu.VMEM((2, 16, channels), f32),
+            pltpu.VMEM((rows, channels), bf16),
+            pltpu.VMEM((rows, channels), bf16),
+            pltpu.VMEM((rows, channels), f32),
+            pltpu.VMEM((rows, channels), bf16),
+            pltpu.VMEM((9 + taps, frames, channels), f32),
+            pltpu.VMEM((2, 4, 2) + wide, bf16),
+            pltpu.VMEM((2, 4) + wide, bf16),
+            pltpu.VMEM((2, 4) + wide, bf16),
+            pltpu.VMEM(wide, f32),
+            pltpu.VMEM((4,) + wide, bf16),
+            pltpu.VMEM((4,) + wide, bf16),
+            pltpu.VMEM((3,) + wide, bf16),
+            pltpu.VMEM((3,) + wide, bf16),
+            pltpu.VMEM((4, 16, channels), f32),
+            pltpu.VMEM((5, 16, channels), f32),
         ]
-        + [dma((n,)) for n in (8, 8, 4, 4, 4, 4, 3, 3, 5, 5)],
-        compiler_params=pltpu.CompilerParams(collective_id=1, has_side_effects=True),
-        name="reduce_grads",
-    )(wg.reshape(2, 4, 2, 2, depth, channels), st)
+        + [dma((n,)) for n in (4, 4, 6, 6, 8, 8, 16, 16, 4)]
+        + [dma((n,)) for n in (8, 8, 8, 8, 4, 4, 3, 3, 5, 5)],
+        compiler_params=pltpu.CompilerParams(
+            collective_id=0, has_side_effects=True, vmem_limit_bytes=48 << 20
+        ),
+        name="whole_backward",
+    )(sess, x, cot, read, w, sk, tk)
 
 
 def local(
     section_inputs, cotangent, sessions, point_weight, spatial_kernel, temporal_kernel, readout
 ):
-    mine = lax.axis_index("section")
     _, clip_count, frames, side, _, channels = section_inputs.shape
     cells = side * side
-    part = clip_count // 2
-    f32 = jnp.float32
 
     def by_cell(block):
         last = block.shape[-1]
         return block.reshape(-1, frames, cells, last).transpose(0, 2, 1, 3).reshape(-1, last)
 
-    taps = temporal_kernel.shape[1]
     halves = by_cell(section_inputs[0]).reshape(2, -1, channels)
-    cot = by_cell(lax.dynamic_slice_in_dim(cotangent, mine * part, part, 0))
-    sess = lax.dynamic_slice_in_dim(sessions, mine * part, part, 0)
-    spare = jnp.zeros((16 - 9 - taps, channels), f32)
-    kernels = jnp.concatenate([spatial_kernel[0], temporal_kernel[0], spare], axis=0)
-    x_both, w_both, k_both = gather_call(halves, point_weight[0], kernels)
-    wg, st = both_call(
-        frames, side, taps, sess, x_both, cot, readout, w_both.reshape(2, channels, channels), k_both
-    )
+    cot = by_cell(cotangent).reshape(2, -1, cotangent.shape[-1])
     factor = 1.0 / math.sqrt(clip_count * lax.axis_size("dp") * frames * cells)
-    grads, small = reduce_call(factor, wg, st)
-    return (grads[None], small[:9][None], small[9 : 9 + taps][None])
+    grads, s_out, t_out = whole_call(
+        frames,
+        side,
+        factor,
+        sessions,
+        halves,
+        cot,
+        readout,
+        point_weight[0],
+        spatial_kernel.transpose(1, 0, 2),
+        temporal_kernel.transpose(1, 0, 2),
+    )
+    return (grads[None], s_out.transpose(1, 0, 2), t_out.transpose(1, 0, 2))
 
 
 def solution(mesh):

time: 87 us -> 68.4 us (0.79)
  local copies, waits for them, and re-layouts: 15.9 us -> 4.92 us
  Pallas kernels: 69.1 us -> 62.5 us
    unnamed x20 -> x13, local copies, waits for them, and re-layouts: 10.4 us -> 1.9 us
    pallas_call x3 -> x1, Pallas kernels: 69.1 us -> 62.5 us  [whole_call(): pl.pallas_call(functools.partial(whole_kernel, frames, side, factor), out...]
    broadcast_in_dim x3 -> x0, local copies, waits for them, and re-layouts: 1.55 us -> none  [the longest x2 1.54 us: local(): return (grads[None], small[:9][None], small[9:9 + taps][None])]
    another operation x1, local copies, waits for them, and re-layouts: 3.07 us -> 2 us  [by_cell(): block.reshape(-1, frames, cells, last).transpose(0, 2, 1, 3)]
    reshape x0 -> x1, local copies, waits for them, and re-layouts: none -> 1.02 us  [by_cell(): block.reshape(-1, frames, cells, last).transpose(0, 2, 1, 3)]
where the time goes in v3:
time: 68.4 us; the launch traced here: 68.1 us
  Pallas kernels  62.5 us (91%)
  local copies, waits for them, and re-layouts  4.92 us (7%)
  between operations  0.72 us (1%)
    pallas_call x1, Pallas kernels, whole_call(): pl.pallas_call(functools.partial(whole_kernel, frames, side, factor), out...  62.5 us
    another operation x1, local copies, waits for them, and re-layouts, by_cell(): block.reshape(-1, frames, cells, last).transpose(0, 2, 1, 3)  2 us
    unnamed x13, local copies, waits for them, and re-layouts  1.9 us

profile of v3, /device:TPU:0, one launch (start us, length us, event | category | flops | bytes accessed | tf_op | source)
XLA Modules:
  0.0 68.1 jit_solution(6951440284351722495)
XLA Ops:
  0.6 1.0 %copy.11 = bf16[8,8,16,128]{3,1,2,0:T(8,128)(2,1)S(1)} copy(bf16[8,8,16,128]{3,2,1,0:T(8,128)(2,1)} %bitcast.23) | data formatting | bytes 524288 | tf_op jit(solution)/shard_map/reshape | solution.py:590
  1.7 0.0 copy-start
  1.7 0.0 copy-start.1
  1.7 0.0 copy-start.2
  1.7 0.0 copy-start.3
  1.7 0.0 copy-start.4
  1.7 2.0 %copy.12 = bf16[1,8,8,4,4,768]{5,2,4,3,1,0:T(8,128)(2,1)S(1)} copy(bf16[1,8,8,4,4,768]{5,4,3,2,1,0:T(4,128)(2,1)} %param.7) | data formatting | bytes 3145728 | tf_op jit(solution)/shard_map/reshape;squeeze | solution.py:590
  3.7 0.0 copy-done
  3.7 0.0 copy-done.1
  3.7 0.0 copy-done.2
  3.7 0.0 copy-done.3
  3.7 0.0 copy-done.4
  3.8 62.5 %whole_backward.1 = (f32[48,768]{1,0:T(8,128)S(1)}, f32[9,1,768]{2,1,0:T(1,128)S(1)}, f32[5,1,768]{2,1,0:T(1,128)S(1)}) custom-call(s32[8]{0:T(128)S(1)} %copy-done.4, bf16[2,512,768]{2,1,0:T(8,128)(2,1)S(1)} %bitcast.15, bf16[2,512,128]{2,1,0:T(8,128)(2,1)S(1)} %bitcast.16, bf16[4,128,768]{2,1,0:T(8,128)(2,1)S(1)} %copy-done, bf16[48,768]{1,0:T(8,128)(2,1)S(1)} %bitcast.18, ...), custom_call_target="tpu_custom_call" | custom-call | tf_op jit(solution)/shard_map/whole_backward/pallas_call | solution.py:541
  66.3 0.7 copy.16
  66.9 0.6 copy.17
  67.5 0.6 copy.18
Async XLA Ops:
  1.7 2.1 %copy-start = (bf16[4,128,768]{2,1,0:T(8,128)(2,1)S(1)}, bf16[4,128,768]{2,1,0:T(8,128)(2,1)}, u32[]{:S(2)}) copy-start(bf16[4,128,768]{2,1,0:T(8,128)(2,1)} %read_ref.1) | copy-start | bytes 2359300
  1.7 2.1 %copy-start.1 = (bf16[1,48,768]{2,1,0:T(8,128)(2,1)S(1)}, bf16[1,48,768]{2,1,0:T(8,128)(2,1)}, u32[]{:S(2)}) copy-start(bf16[1,48,768]{2,1,0:T(8,128)(2,1)} %param.10) | copy-start | bytes 221188
  1.7 2.1 %copy-start.2 = (f32[1,9,768]{2,0,1:T(1,128)S(1)}, f32[1,9,768]{2,0,1:T(1,128)}, u32[]{:S(2)}) copy-start(f32[1,9,768]{2,0,1:T(1,128)} %param.11) | copy-start | bytes 82948
  1.7 2.1 %copy-start.3 = (f32[1,5,768]{2,0,1:T(1,128)S(1)}, f32[1,5,768]{2,0,1:T(1,128)}, u32[]{:S(2)}) copy-start(f32[1,5,768]{2,0,1:T(1,128)} %param.12) | copy-start | bytes 46084
  1.7 2.1 %copy-start.4 = (s32[8]{0:T(128)S(1)}, s32[8]{0:T(128)}, u32[]{:S(2)}) copy-start(s32[8]{0:T(128)} %sess_ref.1) | copy-start | bytes 100

commit v4 on v3

--- a/solution.py
+++ b/solution.py
@@ -207,7 +207,7 @@
 
 def section_work(
     first, frames, side, mine, sess_ref, x_ref, g_in_ref, read_ref, w_ref, sk_ref, tk_ref, wg_ref,
-    st_ref, ing_ref, g_ref, hg_ref, hid_ref, acc_ref, middle
+    st_ref, ing_ref, g_ref, hg_ref, hid_ref, acc_ref, middle, arrive
 ):
     taps = tk_ref.shape[0]
     cells = side * side
@@ -302,12 +302,16 @@
             ).astype(jnp.bfloat16)
         return carry
 
-    if middle is None:
-        lax.fori_loop(0, clips * chunks, step, 0)
-    else:
-        lax.fori_loop(0, clips * chunks // 2, step, 0)
-        middle()
-        lax.fori_loop(clips * chunks // 2, clips * chunks, step, 0)
+
+    def clip_step(clip, carry):
+        arrive(clip)
+        return lax.fori_loop(
+            0, chunks, lambda index, kept: step(clip * chunks + index, kept), carry
+        )
+
+    lax.fori_loop(0, clips // 2, clip_step, 0)
+    middle()
+    lax.fori_loop(clips // 2, clips, clip_step, 0)
     wg = lax.dot_general(
         hid_ref[...], g_ref[...], (((0,), (0,)), ((), ())), preferred_element_type=jnp.float32
     )
@@ -397,8 +401,20 @@
     y_rest = [
         go(sk_ref, sko_ref.at[sec], (ays, ayr), 1, over),
         go(tk_ref, tko_ref.at[sec], (ays, ayr), 2, over),
-        go(x_ref.at[1 - sec], xo_ref.at[sec], (ays, ayr), 3, over),
     ]
+    clip_rows = side * side * frames
+    clips = x_ref.shape[1] // clip_rows
+
+    def clip_copy(clip):
+        span = pl.ds(pl.multiple_of(clip * clip_rows, clip_rows), clip_rows)
+        return remote(
+            x_ref.at[1 - sec, span], xo_ref.at[sec, span], (ays, ayr), 3 + clip, over
+        )
+
+    for clip in range(clips):
+        copy = clip_copy(clip)
+        copy.start()
+        sends.append(copy)
     kept = [
         pltpu.make_async_copy(w_ref, slot_of, own_sem.at[0]),
         pltpu.make_async_copy(sk_ref, sko_ref.at[sec], own_sem.at[1]),
@@ -413,27 +429,48 @@
         z_w[1, h] = go(held, held, (azs, azr), 3 + h, line[h])
     x_w[1, 0] = go(held, held, (axs, axr), 4, side_chip)
     c_w[1, 0] = go(held, held, (acs, acr), 8, mate)
+
+    def slot_copy(s, source, sems, base, h, there):
+        kind = (s + sec) % 2
+        held = wo_ref.at[s, source]
+        return remote(held, held, sems, base * kind + h, there)
+
+    def pass_on(copy):
+        copy.start()
+        sends.append(copy)
+
+    def from_line(s, h):
+        source = (z + 3 - h) % 4 * 4 + x * 2 + c
+        slot_copy(s, source, (azs, azr), 3, h, line[h]).wait_recv()
+        pass_on(slot_copy(s, source, (axs, axr), 4, h + 1, side_chip))
+        pass_on(slot_copy(s, source, (acs, acr), 8, h + 1, mate))
+
+    def from_side(s):
+        for h in range(4):
+            source = (z + 4 - h) % 4 * 4 + (1 - x) * 2 + c
+            slot_copy(s, source, (axs, axr), 4, h, side_chip).wait_recv()
+            pass_on(slot_copy(s, source, (acs, acr), 8, h + 4, mate))
+
+    def from_mate(s):
+        for h in range(8):
+            slot_copy(s, dp, (acs, acr), 8, h, mate).wait_recv()
+
     for h in range(3):
-        source = (z + 3 - h) % 4 * 4 + x * 2 + c
-        for kind in range(2):
-            z_w[kind, h].wait_recv()
-            held = wo_ref.at[secs[kind], source]
-            x_w[kind, h + 1] = go(held, held, (axs, axr), 4 * kind + h + 1, side_chip)
-            c_w[kind, h + 1] = go(held, held, (acs, acr), 8 * kind + h + 1, mate)
-    for h in range(4):
-        source = (z + 4 - h) % 4 * 4 + (1 - x) * 2 + c
-        for kind in range(2):
-            x_w[kind, h].wait_recv()
-            held = wo_ref.at[secs[kind], source]
-            c_w[kind, h + 4] = go(held, held, (acs, acr), 8 * kind + h + 4, mate)
-    for copy in c_w.values():
-        copy.wait_recv()
+        from_line(1, h)
+        from_line(0, h)
+    from_side(1)
+    from_mate(1)
     for copy in y_rest:
         copy.wait_recv()
     for copy in kept:
         copy.wait()
 
     def compute(s, middle):
+        def arrive(clip):
+            @pl.when(sec != s)
+            def _():
+                clip_copy(clip).wait_recv()
+
         ing_ref, g_ref, hg_ref, hid_ref, acc_ref = work
         section_work(
             s == 1,
@@ -455,6 +492,7 @@
             hid_ref,
             acc_ref,
             middle,
+            arrive,
         )
 
     core = {}
@@ -473,8 +511,9 @@
             ).astype(bf16)
             go(xsend.at[s, k], xgot.at[s, k], (xs, xr), 4 * s + k, side_chip)
 
-    compute(1, None)
+    compute(1, lambda: from_side(0))
     core_stage(1)
+    from_mate(0)
     compute(0, lambda: x_stage(1))
     core_stage(0)
     small = [go(st_ref.at[1 - sec], sgot.at[0], (ss, sr), 0, over)]
@@ -534,6 +573,7 @@
     _, rows, channels = x.shape
     depth = w.shape[0]
     taps = tk.shape[0]
+    y_count = 3 + rows // (frames * side * side)
     vmem = pl.BlockSpec(memory_space=pltpu.VMEM)
     dma = pltpu.SemaphoreType.DMA
     bf16, f32 = jnp.bfloat16, jnp.float32
@@ -570,7 +610,7 @@
             pltpu.VMEM((4, 16, channels), f32),
             pltpu.VMEM((5, 16, channels), f32),
         ]
-        + [dma((n,)) for n in (4, 4, 6, 6, 8, 8, 16, 16, 4)]
+        + [dma((n,)) for n in (y_count, y_count, 6, 6, 8, 8, 16, 16, 4)]
         + [dma((n,)) for n in (8, 8, 8, 8, 4, 4, 3, 3, 5, 5)],
         compiler_params=pltpu.CompilerParams(
             collective_id=0, has_side_effects=True, vmem_limit_bytes=48 << 20

time: 68.4 us -> 67.8 us (level)
  no operation moved by 1% of the time
where the time goes in v4:
time: 67.8 us; the launch traced here: 67.6 us
  Pallas kernels  62 us (91%)
  local copies, waits for them, and re-layouts  4.92 us (7%)
  between operations  0.72 us (1%)
    pallas_call x1, Pallas kernels, whole_call(): pl.pallas_call(functools.partial(whole_kernel, frames, side, factor), out...  62 us
    another operation x1, local copies, waits for them, and re-layouts, by_cell(): block.reshape(-1, frames, cells, last).transpose(0, 2, 1, 3)  2 us
    unnamed x13, local copies, waits for them, and re-layouts  1.9 us

profile of v4, /device:TPU:0, one launch (start us, length us, event | category | flops | bytes accessed | tf_op | source)
XLA Modules:
  0.0 67.6 jit_solution(794304692027372291)
XLA Ops:
  0.6 1.0 %copy.11 = bf16[8,8,16,128]{3,1,2,0:T(8,128)(2,1)S(1)} copy(bf16[8,8,16,128]{3,2,1,0:T(8,128)(2,1)} %bitcast.23) | data formatting | bytes 524288 | tf_op jit(solution)/shard_map/reshape | solution.py:630
  1.7 0.0 copy-start
  1.7 0.0 copy-start.1
  1.7 0.0 copy-start.2
  1.7 0.0 copy-start.3
  1.7 0.0 copy-start.4
  1.7 2.0 %copy.12 = bf16[1,8,8,4,4,768]{5,2,4,3,1,0:T(8,128)(2,1)S(1)} copy(bf16[1,8,8,4,4,768]{5,4,3,2,1,0:T(4,128)(2,1)} %param.7) | data formatting | bytes 3145728 | tf_op jit(solution)/shard_map/reshape;squeeze | solution.py:630
  3.7 0.0 copy-done
  3.7 0.0 copy-done.1
  3.7 0.0 copy-done.2
  3.7 0.0 copy-done.3
  3.7 0.0 copy-done.4
  3.8 62.0 %whole_backward.1 = (f32[48,768]{1,0:T(8,128)S(1)}, f32[9,1,768]{2,1,0:T(1,128)S(1)}, f32[5,1,768]{2,1,0:T(1,128)S(1)}) custom-call(s32[8]{0:T(128)S(1)} %copy-done.4, bf16[2,512,768]{2,1,0:T(8,128)(2,1)S(1)} %bitcast.15, bf16[2,512,128]{2,1,0:T(8,128)(2,1)S(1)} %bitcast.16, bf16[4,128,768]{2,1,0:T(8,128)(2,1)S(1)} %copy-done, bf16[48,768]{1,0:T(8,128)(2,1)S(1)} %bitcast.18, ...), custom_call_target="tpu_custom_call" | custom-call | tf_op jit(solution)/shard_map/whole_backward/pallas_call | solution.py:581
  65.7 0.7 copy.16
  66.4 0.6 copy.17
  67.0 0.6 copy.18
Async XLA Ops:
  1.7 2.1 %copy-start = (bf16[4,128,768]{2,1,0:T(8,128)(2,1)S(1)}, bf16[4,128,768]{2,1,0:T(8,128)(2,1)}, u32[]{:S(2)}) copy-start(bf16[4,128,768]{2,1,0:T(8,128)(2,1)} %read_ref.1) | copy-start | bytes 2359300
  1.7 2.1 %copy-start.1 = (bf16[1,48,768]{2,1,0:T(8,128)(2,1)S(1)}, bf16[1,48,768]{2,1,0:T(8,128)(2,1)}, u32[]{:S(2)}) copy-start(bf16[1,48,768]{2,1,0:T(8,128)(2,1)} %param.10) | copy-start | bytes 221188
  1.7 2.1 %copy-start.2 = (f32[1,9,768]{2,0,1:T(1,128)S(1)}, f32[1,9,768]{2,0,1:T(1,128)}, u32[]{:S(2)}) copy-start(f32[1,9,768]{2,0,1:T(1,128)} %param.11) | copy-start | bytes 82948
  1.7 2.1 %copy-start.3 = (f32[1,5,768]{2,0,1:T(1,128)S(1)}, f32[1,5,768]{2,0,1:T(1,128)}, u32[]{:S(2)}) copy-start(f32[1,5,768]{2,0,1:T(1,128)} %param.12) | copy-start | bytes 46084
  1.7 2.1 %copy-start.4 = (s32[8]{0:T(128)S(1)}, s32[8]{0:T(128)}, u32[]{:S(2)}) copy-start(s32[8]{0:T(128)} %sess_ref.1) | copy-start | bytes 100

commit v5 on v4

--- a/solution.py
+++ b/solution.py
@@ -206,7 +206,7 @@
 
 
 def section_work(
-    first, frames, side, mine, sess_ref, x_ref, g_in_ref, read_ref, w_ref, sk_ref, tk_ref, wg_ref,
+    first, frames, side, x_ref, w_ref, sk_ref, tk_ref, wg_ref,
     st_ref, ing_ref, g_ref, hg_ref, hid_ref, acc_ref, middle, arrive
 ):
     taps = tk_ref.shape[0]
@@ -215,14 +215,6 @@
     channels = x_ref.shape[1]
     rows = x_ref.shape[0]
     clips = rows // clip_rows
-    if first:
-        for clip in range(clips):
-            span = pl.ds(clip * clip_rows, clip_rows)
-            g_ref[span, :] = jnp.dot(
-                g_in_ref[mine, span, :],
-                read_ref[sess_ref[mine * clips + clip]],
-                preferred_element_type=jnp.float32,
-            ).astype(jnp.bfloat16)
     hg_ref[...] = lax.dot_general(
         g_ref[...], w_ref[...].reshape(channels, channels), (((1,), (1,)), ((), ())), preferred_element_type=jnp.float32
     )
@@ -455,6 +447,14 @@
         for h in range(8):
             slot_copy(s, dp, (acs, acr), 8, h, mate).wait_recv()
 
+    top_ref = work[1]
+    for clip in range(clips):
+        span = pl.ds(clip * clip_rows, clip_rows)
+        top_ref[span, :] = jnp.dot(
+            cot_ref[sec, span, :],
+            read_ref[sess_ref[sec * clips + clip]],
+            preferred_element_type=jnp.float32,
+        ).astype(bf16)
     for h in range(3):
         from_line(1, h)
         from_line(0, h)
@@ -476,11 +476,7 @@
             s == 1,
             frames,
             side,
-            sec,
-            sess_ref,
             xo_ref.at[s],
-            cot_ref,
-            read_ref,
             wo_ref.at[s],
             sko_ref.at[s],
             tko_ref.at[s],

time: 67.8 us -> 67.6 us (level)
  no operation moved by 1% of the time
where the time goes in v5:
time: 67.6 us; the launch traced here: 67.4 us
  Pallas kernels  61.7 us (91%)
  local copies, waits for them, and re-layouts  4.92 us (7%)
  between operations  0.72 us (1%)
    pallas_call x1, Pallas kernels, whole_call(): pl.pallas_call(functools.partial(whole_kernel, frames, side, factor), out...  61.7 us
    another operation x1, local copies, waits for them, and re-layouts, by_cell(): block.reshape(-1, frames, cells, last).transpose(0, 2, 1, 3)  2 us
    unnamed x13, local copies, waits for them, and re-layouts  1.9 us

profile of v5, /device:TPU:0, one launch (start us, length us, event | category | flops | bytes accessed | tf_op | source)
XLA Modules:
  0.0 67.4 jit_solution(7168174365121997569)
XLA Ops:
  0.6 1.0 %copy.11 = bf16[8,8,16,128]{3,1,2,0:T(8,128)(2,1)S(1)} copy(bf16[8,8,16,128]{3,2,1,0:T(8,128)(2,1)} %bitcast.23) | data formatting | bytes 524288 | tf_op jit(solution)/shard_map/reshape | solution.py:626
  1.7 0.0 copy-start
  1.7 0.0 copy-start.1
  1.7 0.0 copy-start.2
  1.7 0.0 copy-start.3
  1.7 0.0 copy-start.4
  1.7 2.0 %copy.12 = bf16[1,8,8,4,4,768]{5,2,4,3,1,0:T(8,128)(2,1)S(1)} copy(bf16[1,8,8,4,4,768]{5,4,3,2,1,0:T(4,128)(2,1)} %param.7) | data formatting | bytes 3145728 | tf_op jit(solution)/shard_map/reshape;squeeze | solution.py:626
  3.7 0.0 copy-done
  3.7 0.0 copy-done.1
  3.7 0.0 copy-done.2
  3.7 0.0 copy-done.3
  3.7 0.0 copy-done.4
  3.8 61.7 %whole_backward.1 = (f32[48,768]{1,0:T(8,128)S(1)}, f32[9,1,768]{2,1,0:T(1,128)S(1)}, f32[5,1,768]{2,1,0:T(1,128)S(1)}) custom-call(s32[8]{0:T(128)S(1)} %copy-done.4, bf16[2,512,768]{2,1,0:T(8,128)(2,1)S(1)} %bitcast.15, bf16[2,512,128]{2,1,0:T(8,128)(2,1)S(1)} %bitcast.16, bf16[4,128,768]{2,1,0:T(8,128)(2,1)S(1)} %copy-done, bf16[48,768]{1,0:T(8,128)(2,1)S(1)} %bitcast.18, ...), custom_call_target="tpu_custom_call" | custom-call | tf_op jit(solution)/shard_map/whole_backward/pallas_call | solution.py:577
  65.5 0.7 copy.16
  66.1 0.6 copy.17
  66.8 0.6 copy.18
Async XLA Ops:
  1.7 2.1 %copy-start = (bf16[4,128,768]{2,1,0:T(8,128)(2,1)S(1)}, bf16[4,128,768]{2,1,0:T(8,128)(2,1)}, u32[]{:S(2)}) copy-start(bf16[4,128,768]{2,1,0:T(8,128)(2,1)} %read_ref.1) | copy-start | bytes 2359300
  1.7 2.1 %copy-start.1 = (bf16[1,48,768]{2,1,0:T(8,128)(2,1)S(1)}, bf16[1,48,768]{2,1,0:T(8,128)(2,1)}, u32[]{:S(2)}) copy-start(bf16[1,48,768]{2,1,0:T(8,128)(2,1)} %param.10) | copy-start | bytes 221188
  1.7 2.1 %copy-start.2 = (f32[1,9,768]{2,0,1:T(1,128)S(1)}, f32[1,9,768]{2,0,1:T(1,128)}, u32[]{:S(2)}) copy-start(f32[1,9,768]{2,0,1:T(1,128)} %param.11) | copy-start | bytes 82948
  1.7 2.1 %copy-start.3 = (f32[1,5,768]{2,0,1:T(1,128)S(1)}, f32[1,5,768]{2,0,1:T(1,128)}, u32[]{:S(2)}) copy-start(f32[1,5,768]{2,0,1:T(1,128)} %param.12) | copy-start | bytes 46084
  1.7 2.1 %copy-start.4 = (s32[8]{0:T(128)S(1)}, s32[8]{0:T(128)}, u32[]{:S(2)}) copy-start(s32[8]{0:T(128)} %sess_ref.1) | copy-start | bytes 100
